TPU v7x, 256 devices: a whole 4x4x8 slice. The times are simulated.
256 devices in a mesh: obs: 32 (over x, y, core), row: 8 (over z).
Axes of the slice: x: 4, y: 4, z: 8, core: 2. Of those that a mesh axis runs over, the one named last changes fastest.
Arguments:
- camera_jacobian: float32 [18, 262144], P(None, ('obs', 'row')), may hold values from -0.75 to 0.75
- point_jacobian: float32 [6, 262144], P(None, ('obs', 'row')), may hold values from -6 to 6
- residual: float32 [2, 262144], P(None, ('obs', 'row')), may hold values from -6 to 6
- send_order: int32 [262144], P(('obs', 'row')), may hold values from 0 to 1023, as said below
- camera_of: int32 [262144], P(('obs', 'row')), may hold values from 0 to 127, as said below
- track_of: int32 [262144], P(('obs', 'row')), may hold values from 0 to 511, as said below
- partner: int32 [7, 262144], P(None, ('obs', 'row')), may hold values from 0 to 1023, as said below
- pair_slot: int32 [7, 262144], P(None, ('obs', 'row')), may hold values from 0 to 1792, as said below
Outputs:
- camera_hessian: float32 [81, 4096], P(None, ('obs', 'row'))
- camera_gradient: float32 [9, 4096], P(None, ('obs', 'row'))
- pair_hessian: float32 [81, 57344], P(None, ('obs', 'row'))
Inputs may be any that keep to these rules, and one draw needn't show every extreme that they name: `send_order`: on each device a permutation of the device's 1024 observations. `camera_of`: A device's observations are ordered by camera. `track_of`: local track of each received slot of one track owner; a track has 2 to 8 observations, at most one from each source obs index, from cyclically consecutive source obs indices; some track ids are unused. partner[k] of a received slot is the slot of the k-th other observation of its track in track order, or the slot itself where the track has fewer than k + 2 observations. pair_slot[k] of a send slot is c * 14 + o, where c is the observation's camera and o encodes its partner's camera; 1792 exactly where partner[k] is the slot itself.
All inputs are finite; a program needn't handle non-finite values.
Results may differ from a plain program's by a relative error of at most 0.00014.
Values sent between devices are 32-bit elements; how exact they have to be, the bound alone decides.
No kernel may reach another device: no remote copies, remote signals or barrier semaphores. Data moves between devices by JAX's collectives and lax.ppermute only.
A program may use at most 64 MiB of HBM per device.

v0:
```python
import jax
import jax.numpy as jnp
from jax import lax
from jax.sharding import PartitionSpec as P

CAM_ROW = 16
NBR = 14


damping = 1.0


def eliminate(camera_rows, point_rows, resid_rows, track_of, track_count):
    camera = camera_rows.reshape(2, 9, -1)
    point_jac = point_rows.reshape(2, 3, -1)
    normal = jnp.stack(
        [
            point_jac[0, 0] * point_jac[0, 0] + point_jac[1, 0] * point_jac[1, 0],
            point_jac[0, 0] * point_jac[0, 1] + point_jac[1, 0] * point_jac[1, 1],
            point_jac[0, 0] * point_jac[0, 2] + point_jac[1, 0] * point_jac[1, 2],
            point_jac[0, 1] * point_jac[0, 1] + point_jac[1, 1] * point_jac[1, 1],
            point_jac[0, 1] * point_jac[0, 2] + point_jac[1, 1] * point_jac[1, 2],
            point_jac[0, 2] * point_jac[0, 2] + point_jac[1, 2] * point_jac[1, 2],
            point_jac[0, 0] * resid_rows[0] + point_jac[1, 0] * resid_rows[1],
            point_jac[0, 1] * resid_rows[0] + point_jac[1, 1] * resid_rows[1],
            point_jac[0, 2] * resid_rows[0] + point_jac[1, 2] * resid_rows[1],
        ]
    )
    totals = jnp.zeros((9, track_count), jnp.float32).at[:, track_of].add(normal)
    pivot_first = jnp.sqrt(totals[0] + damping)
    lower_one = totals[1] / pivot_first
    lower_two = totals[2] / pivot_first
    pivot_second = jnp.sqrt(totals[3] + damping - lower_one * lower_one)
    lower_mid = (totals[4] - lower_two * lower_one) / pivot_second
    pivot_third = jnp.sqrt(totals[5] + damping - lower_two * lower_two - lower_mid * lower_mid)
    solved_one = totals[6] / pivot_first
    solved_two = (totals[7] - lower_one * solved_one) / pivot_second
    solved_three = (totals[8] - lower_two * solved_one - lower_mid * solved_two) / pivot_third
    per_track = jnp.stack(
        [
            pivot_first,
            lower_one,
            lower_two,
            pivot_second,
            lower_mid,
            pivot_third,
            solved_one,
            solved_two,
            solved_three,
        ]
    )
    per_obs = per_track[:, track_of]
    weights = (
        camera[0][:, None, :] * point_jac[0][None, :, :]
        + camera[1][:, None, :] * point_jac[1][None, :, :]
    )
    column_one = weights[:, 0] / per_obs[0]
    column_two = (weights[:, 1] - per_obs[1] * column_one) / per_obs[3]
    column_three = (weights[:, 2] - per_obs[2] * column_one - per_obs[4] * column_two) / per_obs[5]
    factor = jnp.stack([column_one, column_two, column_three])
    point_shift = column_one * per_obs[6] + column_two * per_obs[7] + column_three * per_obs[8]
    return (factor, point_shift)


def camera_terms(camera_rows, resid_rows, factor, point_shift):
    camera = camera_rows.reshape(2, 9, -1)
    normal = (
        camera[0][:, None, :] * camera[0][None, :, :]
        + camera[1][:, None, :] * camera[1][None, :, :]
    )
    schur_part = (
        factor[0][:, None, :] * factor[0][None, :, :]
        + factor[1][:, None, :] * factor[1][None, :, :]
        + factor[2][:, None, :] * factor[2][None, :, :]
    )
    gradient = camera[0] * resid_rows[0] + camera[1] * resid_rows[1] - point_shift
    return jnp.concatenate([(normal - schur_part).reshape(81, -1), gradient], axis=0)


def pair_product(left, right):
    total = (
        left[0][:, None] * right[0][None, :]
        + left[1][:, None] * right[1][None, :]
        + left[2][:, None] * right[2][None, :]
    )
    return -total.reshape(81, -1)


def on_device(
    camera_jacobian, point_jacobian, residual, send_order, camera_of, track_of, partner, pair_slot
):
    obs_count = camera_jacobian.shape[1]
    ranks = partner.shape[0]
    camera_count = CAM_ROW * lax.axis_size("row")
    slot_count = camera_count * NBR
    stacked = jnp.concatenate([camera_jacobian, point_jacobian, residual], axis=0)
    sent = jnp.take(stacked, send_order, axis=1)
    owned = lax.all_to_all(sent, "obs", split_axis=1, concat_axis=1, tiled=True)
    factor, point_shift = eliminate(
        owned[:18], owned[18:24], owned[24:26], track_of, obs_count // 2
    )
    flat_factor = factor.reshape(27, obs_count)
    chosen = jnp.take(flat_factor, partner.reshape(-1), axis=1)
    back = lax.all_to_all(
        jnp.concatenate([flat_factor, point_shift], axis=0),
        "obs",
        split_axis=1,
        concat_axis=1,
        tiled=True,
    )
    block_values = pair_product(factor[:, :, None, :], chosen.reshape(3, 9, ranks, obs_count))
    arrived = lax.all_to_all(
        block_values.reshape(81, ranks, obs_count), "obs", split_axis=2, concat_axis=2, tiled=True
    ).reshape(81, ranks * obs_count)
    factor_back = back[:27].reshape(3, 9, obs_count)
    shift_back = back[27:]
    local_terms = camera_terms(sent[:18], sent[24:26], factor_back, shift_back)
    camera_ids = jnp.take(camera_of, send_order)
    indicator = (camera_ids[:, None] == jnp.arange(camera_count, dtype=jnp.int32)[None, :]).astype(
        jnp.float32
    )
    camera_partial = jnp.dot(
        local_terms, indicator, precision=lax.Precision.HIGHEST, preferred_element_type=jnp.float32
    )
    camera_mine = lax.psum_scatter(camera_partial, "row", scatter_dimension=1, tiled=True)
    pair_total = (
        jnp.zeros((81, slot_count + 1), jnp.float32).at[:, pair_slot.reshape(-1)].add(arrived)
    )
    pair_mine = lax.psum_scatter(pair_total[:, :slot_count], "row", scatter_dimension=1, tiled=True)
    return (camera_mine[:81], camera_mine[81:], pair_mine)


def solution(mesh):
    return jax.shard_map(
        on_device,
        mesh=mesh,
        in_specs=(
            P(None, ("obs", "row")),
            P(None, ("obs", "row")),
            P(None, ("obs", "row")),
            P(("obs", "row")),
            P(("obs", "row")),
            P(("obs", "row")),
            P(None, ("obs", "row")),
            P(None, ("obs", "row")),
        ),
        out_specs=(P(None, ("obs", "row")), P(None, ("obs", "row")), P(None, ("obs", "row"))),
        check_vma=False,
    )
```

profile of v0, /device:TPU:1, one launch (start us, length us, event | category | flops | bytes accessed | tf_op | source)
XLA Modules:
  0.0 264.4 jit_solution(3819457355490105620)
XLA Ops:
  7.2 0.7 fusion.18
  8.0 4.5 %gather_fusion.2 = s32[1024]{0:T(1024)S(1)} fusion(s32[1024]{0:T(1024)S(1)} %copy-done, s32[1024]{0:T(1024)S(1)} %fusion.18), kind=kCustom, calls=%fused_computation.2 | custom fusion | bytes 12288 | tf_op jit(solution)/shard_map/jit(_take)/gather | solution.py:118
  12.5 0.6 broadcast_select_fusion.1
  13.2 0.2 copy.247
  13.4 2.8 %gather_fusion = f32[1024,26]{1,0:T(8,128)S(1)} fusion(f32[26,1024]{0,1:T(8,128)S(1)} %copy.247, s32[1024]{0:T(1024)S(1)} %fusion.18), kind=kCustom, calls=%fused_computation | custom fusion | bytes 217088 | tf_op jit(solution)/shard_map/jit(_take)/gather | solution.py:97
  16.6 0.3 fusion.39
  16.9 0.9 reshape.994
  17.8 8.6 %all-to-all-start = ((f32[32,1,832]{2,1,0:T(1,128)}), f32[32,1,832]{2,1,0:T(1,128)S(1)}, u32[]{:S(2)}, u32[]{:S(2)}) async-start(f32[32,1,832]{2,1,0:T(1,128)} %reshape.994), calls=%async_computation | async-start | bytes 229376 | tf_op jit(solution)/shard_map/all_to_all | solution.py:98
  26.4 0.6 copy-done.1
  27.1 0.6 fusion.38
  27.9 6.1 %all-to-all-done = f32[32,1,832]{2,1,0:T(1,128)S(1)} async-done(((f32[32,1,832]{2,1,0:T(1,128)}), f32[32,1,832]{2,1,0:T(1,128)S(1)}, u32[]{:S(2)}, u32[]{:S(2)}) %all-to-all-start) | async-done | bytes 106528 | tf_op jit(solution)/shard_map/all_to_all | solution.py:98
  33.9 0.6 broadcast.412
  34.5 0.9 reduce.32
  36.9 0.2 copy.255
  37.1 6.1 %scatter_custom_fusion = f32[9,512]{0,1:T(8,128)S(1)} fusion(s32[1024]{0:T(1024)S(1)} %get-tuple-element.93, f32[1024,9]{1,0:T(8,128)S(1)} %copy.255, f32[]{:T(128)} %constant.34.clone.1), kind=kCustom, calls=%fused_computation.39 | custom fusion | flops 9216 | bytes 18436 | tf_op jit(solution)/shard_map/scatter-add | solution.py:29
  43.2 0.6 fusion.35
  45.2 2.8 %gather_fusion.1 = f32[1024,9]{1,0:T(8,128)S(1)} fusion(f32[9,512]{0,1:T(8,128)S(1)} %copy.265, s32[1024]{0:T(1024)S(1)} %get-tuple-element.92), kind=kCustom, calls=%fused_computation.1 | custom fusion | bytes 77824 | tf_op jit(solution)/shard_map/gather | solution.py:52
  48.0 2.4 slice_reduce_fusion.8
  51.7 0.5 copy.266
  52.2 1.2 reshape.996
  53.4 3.9 %all-to-all-start.1 = ((f32[32,1,1152]{2,1,0:T(1,128)}), f32[32,1,1152]{2,1,0:T(1,128)S(1)}, u32[]{:S(2)}, u32[]{:S(2)}) async-start(f32[32,1,1152]{2,1,0:T(1,128)} %reshape.996), calls=%async_computation.1 | async-start | bytes 294912 | tf_op jit(solution)/shard_map/all_to_all | solution.py:104
  57.4 0.2 copy.274
  57.6 24.2 %gather_fusion.3 = f32[7168,27]{1,0:T(8,128)} fusion(f32[27,1024]{0,1:T(8,128)S(1)} %copy.274, s32[7168]{0:T(1024)S(1)} %broadcast_clamp_fusion), kind=kCustom, calls=%fused_computation.3 | custom fusion | bytes 1576960 | tf_op jit(solution)/shard_map/jit(_take)/gather | solution.py:103
  81.8 5.6 %select_bitcast_fusion = f32[27,7168]{0,1:T(8,128)S(1)} fusion(f32[7168,27]{1,0:T(8,128)} %gather_fusion.3, pred[7168]{0:T(1024)(128)(4,1)S(1)} %compare_and_fusion), kind=kLoop, calls=%fused_computation.6 | loop fusion | flops 193536 | bytes 1555456 | tf_op jit(solution)/shard_map/jit(_take)/select_n | solution.py:103
  87.3 6.0 %fusion.31 = (f32[9,7168]{0,1:T(8,128)}, f32[9,7168]{0,1:T(8,128)}, f32[9,7168]{0,1:T(8,128)}) fusion(f32[27,7168]{0,1:T(8,128)S(1)} %select_bitcast_fusion), kind=kLoop, calls=%fused_computation.99 | loop fusion | bytes 1548288 | tf_op jit(solution)/shard_map/slice | solution.py:82
  93.3 3.4 %copy.277 = f32[9,7,1024]{2,1,0:T(8,128)} copy(f32[9,7,1024]{0,2,1:T(8,128)} %bitcast.149) | data formatting | bytes 516096 | tf_op jit(solution)/shard_map/mul | solution.py:84
  96.9 3.4 %copy.276 = f32[9,7,1024]{2,1,0:T(8,128)} copy(f32[9,7,1024]{0,2,1:T(8,128)} %bitcast.148) | data formatting | bytes 516096 | tf_op jit(solution)/shard_map/mul | solution.py:83
  100.5 3.4 %copy.275 = f32[9,7,1024]{2,1,0:T(8,128)} copy(f32[9,7,1024]{0,2,1:T(8,128)} %bitcast.147) | data formatting | bytes 516096 | tf_op jit(solution)/shard_map/mul | solution.py:82
  103.9 0.8 mul.639
  104.7 2.1 fusion.1
  106.8 3.5 %copy.278 = f32[81,7,1024]{0,1,2:T(8,128)} copy(f32[81,7,1024]{2,1,0:T(8,128)S(1)} %fusion.1) | data formatting | bytes 4644864 | tf_op jit(solution)/shard_map/neg | solution.py:86
  110.3 7.5 %all-to-all-start.2 = ((f32[81,7,1024]{0,1,2:T(8,128)}), f32[81,7,1024]{0,1,2:T(8,128)}, u32[]{:S(2)}, u32[]{:S(2)}) async-start(f32[81,7,1024]{0,1,2:T(8,128)} %copy.278), calls=%async_computation.3 | async-start | bytes 8388608 | tf_op jit(solution)/shard_map/all_to_all | solution.py:112
  117.9 1.0 reduce.33
  118.9 0.6 reshape.997
  119.5 0.5 fusion.32
  121.1 1.4 fusion.3
  122.5 0.3 reduce-scatter.5.cloned.1.call-start
  122.8 47.1 %all-to-all-done.2 = f32[81,7,1024]{0,1,2:T(8,128)} async-done(((f32[81,7,1024]{0,1,2:T(8,128)}), f32[81,7,1024]{0,1,2:T(8,128)}, u32[]{:S(2)}, u32[]{:S(2)}) %all-to-all-start.2) | async-done | bytes 2322464 | tf_op jit(solution)/shard_map/all_to_all | solution.py:112
  169.9 3.9 %copy.279 = f32[81,7,1024]{2,1,0:T(8,128)S(1)} copy(f32[81,7,1024]{0,1,2:T(8,128)} %all-to-all-done.2) | data formatting | bytes 4644864 | tf_op jit(solution)/shard_map/all_to_all | solution.py:112
  173.9 0.3 pad.14
  174.1 1.7 copy.295
  175.8 2.6 copy.280
  178.4 40.5 %scatter_custom_fusion.1 = f32[81,1793]{0,1:T(8,128)S(1)} fusion(s32[7168]{0:T(1024)S(1)} %bitcast.169, f32[7168,81]{1,0:T(8,128)} %copy.280, f32[]{:T(128)} %constant.34.clone.1), kind=kCustom, calls=%fused_computation.27 | custom fusion | flops 580608 | bytes 581444 | tf_op jit(solution)/shard_map/scatter-add | solution.py:127
  218.9 1.0 slice.339
  219.9 0.8 slice.335
  220.7 0.7 copy.281
  221.4 34.5 %reduce-scatter.5.cloned.1.call-done = f32[81,224]{0,1:T(8,128)} async-done(((f32[81,1792]{0,1:T(8,128)}), f32[81,224]{0,1:T(8,128)}) %reduce-scatter.5.cloned.1.call-update) | async-done | bytes 72592 | tf_op jit(solution)/shard_map/reduce_scatter | solution.py:129
  255.9 1.6 copy.282
  (109 shorter events, 6.1 us)
Async XLA Ops:
  7.2 0.8 copy-start
  7.2 5.3 %copy-start.9 = (s32[1024]{0:T(1024)S(1)}, s32[1024]{0:T(1024)}, u32[]{:S(2)}) copy-start(s32[1024]{0:T(1024)} %param.11) | copy-start | bytes 12292
  7.2 5.9 %copy-start.10 = (f32[2,1024]{1,0:T(2,128)S(1)}, f32[2,1024]{1,0:T(2,128)}, u32[]{:S(2)}) copy-start(f32[2,1024]{1,0:T(2,128)} %param.10) | copy-start | bytes 24580
  7.2 5.9 %copy-start.5 = (f32[6,1024]{1,0:T(8,128)S(1)}, f32[6,1024]{1,0:T(8,128)}, u32[]{:S(2)}) copy-start(f32[6,1024]{1,0:T(8,128)} %param.9) | copy-start | bytes 73732
  7.2 5.9 %copy-start.4 = (f32[18,1024]{1,0:T(8,128)S(1)}, f32[18,1024]{1,0:T(8,128)}, u32[]{:S(2)}) copy-start(f32[18,1024]{1,0:T(8,128)} %param.8) | copy-start | bytes 221188
  12.5 15.2 %copy-start.3 = (s32[7,1024]{1,0:T(8,128)S(1)}, s32[7,1024]{1,0:T(8,128)}, u32[]{:S(2)}) copy-start(s32[7,1024]{1,0:T(8,128)} %param.14) | copy-start | bytes 86020
  12.5 15.3 %copy-start.11 = (s32[1024]{0:T(1024)S(1)}, s32[1024]{0:T(1024)}, u32[]{:S(2)}) copy-start(s32[1024]{0:T(1024)} %param.13) | copy-start | bytes 12292
  12.5 15.3 %copy-start.6 = (s32[7,1024]{1,0:T(8,128)S(1)}, s32[7,1024]{1,0:T(8,128)}, u32[]{:S(2)}) copy-start(s32[7,1024]{1,0:T(8,128)} %param.15) | copy-start | bytes 86020
  17.8 16.1 %all-to-all-start = ((f32[32,1,832]{2,1,0:T(1,128)}), f32[32,1,832]{2,1,0:T(1,128)S(1)}, u32[]{:S(2)}, u32[]{:S(2)}) async-start(f32[32,1,832]{2,1,0:T(1,128)} %reshape.994), calls=%async_computation | async-start | bytes 229376 | tf_op jit(solution)/shard_map/all_to_all | solution.py:98
  26.4 0.6 copy-start.1
  53.4 56.8 %all-to-all-start.1 = ((f32[32,1,1152]{2,1,0:T(1,128)}), f32[32,1,1152]{2,1,0:T(1,128)S(1)}, u32[]{:S(2)}, u32[]{:S(2)}) async-start(f32[32,1,1152]{2,1,0:T(1,128)} %reshape.996), calls=%async_computation.1 | async-start | bytes 294912 | tf_op jit(solution)/shard_map/all_to_all | solution.py:104
  110.3 59.7 %all-to-all-start.2 = ((f32[81,7,1024]{0,1,2:T(8,128)}), f32[81,7,1024]{0,1,2:T(8,128)}, u32[]{:S(2)}, u32[]{:S(2)}) async-start(f32[81,7,1024]{0,1,2:T(8,128)} %copy.278), calls=%async_computation.3 | async-start | bytes 8388608 | tf_op jit(solution)/shard_map/all_to_all | solution.py:112
  117.8 102.1 %reduce-scatter.3.cloned.1.call-start = ((), (), s32[]{:S(2)}) async-start(), calls=%async_computation.5 | async-start | bytes 73728 | tf_op jit(solution)/shard_map/reduce_scatter | solution.py:125
  118.9 1.9 copy-start.2
  118.9 1.9 copy-start.7
  118.9 1.9 copy-start.8
  119.5 1.6 copy-start.12
  122.5 133.4 %reduce-scatter.5.cloned.1.call-start = ((), (), s32[]{:S(2)}) async-start(), calls=%async_computation.6 | async-start | bytes 1032192 | tf_op jit(solution)/shard_map/reduce_scatter | solution.py:129
Sparse Core Ops, SparseCore 0:
  122.6 35.8 reduce-scatter.2
  220.0 35.8 reduce-scatter.4
where the time goes:
time: 269 us; the launch traced here: 264 us
  waiting for transfers between devices  87.8 us (33%)
  local copies, waits for them, and re-layouts  81.8 us (30%)
  other arithmetic  58.4 us (22%)
  starting transfers between devices  20.3 us (8%)
  between operations  14.7 us (5%)
    all_to_all x1, waiting for transfers between devices, on_device(): lax.all_to_all(block_values.reshape(81, ranks, obs_count), 'obs', split_a...  47.1 us
    scatter-add x1, other arithmetic, on_device(): jnp.zeros((81, slot_count + 1), jnp.float32).at[:, pair_slot.reshape(-1)]  40.5 us
    reduce_scatter x1, waiting for transfers between devices, on_device(): lax.psum_scatter(pair_total[:, :slot_count], 'row', scatter_dimension=1,...  34.5 us
    gather x1, local copies, waits for them, and re-layouts, on_device(): chosen = jnp.take(flat_factor, partner.reshape(-1), axis=1)  24.2 us
    unnamed x45, local copies, waits for them, and re-layouts  9 us
    all_to_all x1, starting transfers between devices, on_device(): owned = lax.all_to_all(sent, 'obs', split_axis=1, concat_axis=1, tiled=True)  8.58 us
    all_to_all x1, starting transfers between devices, on_device(): lax.all_to_all(block_values.reshape(81, ranks, obs_count), 'obs', split_a...  7.55 us
    scatter-add x1, other arithmetic, eliminate(): jnp.zeros((9, track_count), jnp.float32).at[:, track_of].add(normal)  6.09 us
  transfers between devices with their start and end apart: 5, of which 3 were waited for; matrix products, arithmetic and copies ran while one was open for 41% of the time, Pallas kernels for 0%

commit v1 on v0

v1 whole, which is shorter than its diff:
```python
import jax
import jax.numpy as jnp
from jax import lax
from jax.experimental import pallas as pl
from jax.experimental.pallas import tpu as pltpu
from jax.sharding import PartitionSpec as P

CAM_ROW = 16
NBR = 14
RANKS = 7
LANES = 128
GROUP = 32
SLOTS = 1024
CHUNKS = SLOTS // LANES
ROWS_IN = 8
ROWS_BACK = 40
USED_BACK = 33
SIDE = 144
BLOCK = 176
damping = 1.0
F32 = jnp.float32
BF16 = jnp.bfloat16


def lane_groups():
    return lax.broadcasted_iota(jnp.int32, (8, LANES), 1) // GROUP


def regroup(parts, group, sign):
    outs = []
    for a in range(4):
        out = parts[a]
        for b in range(4):
            if b != a:
                out = jnp.where(group == b, pltpu.roll(parts[b], ((b - a) * GROUP) % LANES, 1), out)
        outs.append(out)
    return outs


def pack_kernel(jc, jp, err, cam, order, msg, own, rows):
    rows[0:18, :] = jc[...]
    rows[18:24, :] = jp[...]
    rows[24:26, :] = err[...]
    rows[26:27, :] = cam[...].astype(F32)
    rows[27:32, :] = jnp.zeros((5, SLOTS), F32)
    group = lane_groups()

    def chunk(d, _):
        at = pl.multiple_of(d * LANES, LANES)
        idx = jnp.broadcast_to(order[0:1, pl.ds(at, LANES)], (8, LANES))
        part = idx // LANES
        lane = idx % LANES
        tiles = []
        for t in range(4):
            acc = jnp.zeros((8, LANES), F32)
            for s in range(CHUNKS):
                got = jnp.take_along_axis(rows[t * 8 : t * 8 + 8, s * LANES : (s + 1) * LANES], lane, axis=1)
                acc = jnp.where(part == s, got, acc)
            own[t * 8 : t * 8 + 8, pl.ds(at, LANES)] = acc
            tiles.append(acc)
        for m, tile in enumerate(regroup(tiles, group, 1)):
            msg[pl.ds(pl.multiple_of((d * 4 + m) * ROWS_IN, 8), 8), :] = tile
        return 0

    lax.fori_loop(0, CHUNKS, chunk, 0)


ROLLS = (0, 1, 2, 6, 7)


def owner_kernel(owned, partner, msg, slots, turned, near, back):
    group = lane_groups()
    for r in range(8):
        slots[pl.ds(r, RANKS, stride=8), :] = partner[:, r * LANES : (r + 1) * LANES]
    for row in range(ROWS_IN):
        ins = [owned[pl.ds(m * ROWS_IN + row, 8, stride=4 * ROWS_IN), :] for m in range(4)]
        for t, tile in enumerate(regroup(ins, group, 1)):
            u = t * 8 + row
            if u < 26:
                for n, d in enumerate(ROLLS):
                    turned[n * 26 + u] = tile if d == 0 else pltpu.roll(tile, 8 - d, 0)
    here = lax.broadcasted_iota(jnp.int32, (8, LANES), 0)
    self_slot = here * LANES + lax.broadcasted_iota(jnp.int32, (8, LANES), 1)

    def picks(k):
        idx = slots[pl.ds(pl.multiple_of(k * 8, 8), 8), :]
        step = (idx // LANES - here) % 8
        return idx != self_slot, idx % LANES, [step == d for d in ROLLS]

    def pick(u, lane, masks):
        out = jnp.take_along_axis(turned[u], lane, axis=1)
        for n in range(1, len(ROLLS)):
            out = jnp.where(masks[n], jnp.take_along_axis(turned[n * 26 + u], lane, axis=1), out)
        return out

    def normal(p, e):
        out = []
        for a in range(3):
            for b in range(a, 3):
                out.append(p[a] * p[b] + p[3 + a] * p[3 + b])
        for a in range(3):
            out.append(p[a] * e[0] + p[3 + a] * e[1])
        return out

    mine = [turned[18 + n] for n in range(8)]

    def first(k, total):
        valid, lane, masks = picks(k)
        got = [jnp.where(valid, pick(18 + n, lane, masks), 0.0) for n in range(8)]
        for n in range(6):
            near[k * 6 + n] = got[n]
        return tuple(x + y for x, y in zip(total, normal(got[:6], got[6:])))

    v00, v01, v02, v11, v12, v22, b0, b1, b2 = lax.fori_loop(0, RANKS, first, tuple(normal(mine[:6], mine[6:])))
    i0 = 1.0 / jnp.sqrt(v00 + damping)
    l10 = v01 * i0
    l20 = v02 * i0
    i1 = 1.0 / jnp.sqrt(v11 + damping - l10 * l10)
    l21 = (v12 - l20 * l10) * i1
    i2 = 1.0 / jnp.sqrt(v22 + damping - l20 * l20 - l21 * l21)

    def forward(x0, x1, x2):
        y0 = x0 * i0
        y1 = (x1 - l10 * y0) * i1
        y2 = (x2 - l20 * y0 - l21 * y1) * i2
        return y0, y1, y2

    def inner(x, y):
        return x[0] * y[0] + x[1] * y[1] + x[2] * y[2]

    h = forward(b0, b1, b2)
    g = [forward(*mine[0:3]), forward(*mine[3:6])]
    back[126] = inner(g[0], g[0])
    back[127] = inner(g[0], g[1])
    back[128] = inner(g[1], g[1])
    back[129] = inner(g[0], h)
    back[130] = inner(g[1], h)
    back[131] = jnp.zeros((8, LANES), F32)

    def second(k, _):
        valid, lane, masks = picks(k)
        p = [near[k * 6 + n] for n in range(6)]
        o = [forward(*p[0:3]), forward(*p[3:6])]
        mix = [[-inner(g[a], o[b]) for b in range(2)] for a in range(2)]
        for q in range(9):
            c0 = pick(q, lane, masks)
            c1 = pick(9 + q, lane, masks)
            for a in range(2):
                back[k * 18 + a * 9 + q] = mix[a][0] * c0 + mix[a][1] * c1
        return 0

    lax.fori_loop(0, RANKS, second, 0)

    def emit(row, _):
        tiles = [back[row * 4 + t] for t in range(4)]
        for m, tile in enumerate(regroup(tiles, group, 1)):
            msg[pl.ds(m * ROWS_BACK + row, 8, stride=4 * ROWS_BACK), :] = tile
        return 0

    lax.fori_loop(0, USED_BACK, emit, 0)


def build_right(back, own, pair_slot, right_hi, right_lo, flat):
    group = lane_groups()
    low = lax.broadcasted_iota(jnp.int32, (8, LANES), 0)
    offsets = [low, low + 8]

    def chunk(d, _):
        at = pl.multiple_of(d * LANES, LANES)
        for b in range(ROWS_BACK // 8):
            ins = [back[pl.ds(pl.multiple_of((d * 4 + m) * ROWS_BACK + b * 8, 8), 8), :] for m in range(4)]
            for t, tile in enumerate(regroup(ins, group, 1)):
                flat[t * ROWS_BACK + b * 8 : t * ROWS_BACK + b * 8 + 8, :] = tile

        def spread(u):
            row = (u % 4) * ROWS_BACK + u // 4
            return jnp.broadcast_to(flat[row : row + 1, :], (8, LANES))

        def mine(u):
            return jnp.broadcast_to(own[u : u + 1, pl.ds(at, LANES)], (8, LANES))

        cam = mine(26).astype(jnp.int32)
        hits = []
        for k in range(RANKS):
            slot = jnp.broadcast_to(pair_slot[k : k + 1, pl.ds(at, LANES)], (8, LANES))
            o = jnp.where(slot == CAM_ROW * 8 * NBR, -1, slot - cam * NBR)
            hits.append([o == off for off in offsets])
        m00, m01, m11 = spread(126), spread(127), spread(128)
        grad = [mine(24) - spread(129), mine(25) - spread(130)]
        for q in range(9):
            c0, c1 = mine(q), mine(9 + q)
            diag = [c0 - m00 * c0 - m01 * c1, c1 - m01 * c0 - m11 * c1]
            for i in range(2):
                halves = [jnp.zeros((8, LANES), F32), jnp.where(low == 6, diag[i], 0.0)]
                if q == 0:
                    halves[1] = jnp.where(low == 7, grad[i], halves[1])
                for k in range(RANKS):
                    n = spread(k * 18 + i * 9 + q)
                    halves = [x + jnp.where(hit, n, 0.0) for x, hit in zip(halves, hits[k])]
                value = jnp.concatenate(halves, axis=0)
                hi = value.astype(BF16)
                at2 = pl.multiple_of(d * 2 * LANES + i * LANES, LANES)
                right_hi[q * 16 : q * 16 + 16, pl.ds(at2, LANES)] = hi
                right_lo[q * 16 : q * 16 + 16, pl.ds(at2, LANES)] = (value - hi.astype(F32)).astype(BF16)
        return 0

    lax.fori_loop(0, CHUNKS, chunk, 0)


def dot_t(x, y):
    return lax.dot_general(x, y, (((1,), (1,)), ((), ())), preferred_element_type=F32)


def build_block(dest, own, right_hi, right_lo, left_hi, left_lo, wide, out, base):
    low = lax.broadcasted_iota(jnp.int32, (16, LANES), 0).astype(F32) + (dest * CAM_ROW).astype(F32)

    def chunk(d, _):
        at = pl.multiple_of(d * LANES, LANES)
        hit = jnp.broadcast_to(own[26:27, pl.ds(at, LANES)], (16, LANES)) == low
        for i in range(2):
            at2 = pl.multiple_of(d * 2 * LANES + i * LANES, LANES)
            for p in range(9):
                u = i * 9 + p
                value = jnp.broadcast_to(own[u : u + 1, pl.ds(at, LANES)], (16, LANES))
                value = jnp.where(hit, value, 0.0)
                hi = value.astype(BF16)
                left_hi[p * 16 : p * 16 + 16, pl.ds(at2, LANES)] = hi
                left_lo[p * 16 : p * 16 + 16, pl.ds(at2, LANES)] = (value - hi.astype(F32)).astype(BF16)
        return 0

    lax.fori_loop(0, CHUNKS, chunk, 0)
    total = dot_t(left_hi[...], right_hi[...]) + (
        dot_t(left_hi[...], right_lo[...]) + dot_t(left_lo[...], right_hi[...])
    )
    out[base : base + SIDE, :] = total[:, :LANES]
    wide[:, 0:16] = total[:, LANES:]
    lane = lax.broadcasted_iota(jnp.int32, (16, LANES), 1)
    tail = wide[0:16, :]
    for p in range(1, 8):
        tail = jnp.where(lane // 16 == p, pltpu.roll(wide[p * 16 : p * 16 + 16, :], p * 16, 1), tail)
    out[base + SIDE : base + SIDE + 16, :] = tail
    out[base + SIDE + 16 : base + BLOCK, :] = wide[128:144, :]


def camera_kernel(back, own, pair_slot, out, right_hi, right_lo, left_hi, left_lo, wide, flat):
    build_right(back, own, pair_slot, right_hi, right_lo, flat)
    wide[...] = jnp.zeros((SIDE, LANES), F32)
    for dest in range(8):
        build_block(jnp.int32(dest), own, right_hi, right_lo, left_hi, left_lo, wide, out, dest * BLOCK)


def final_kernel(parts, hess, grad, pair, body, last, rows):
    total = parts[0:BLOCK, :]
    for n in range(1, 8):
        total = total + parts[n * BLOCK : (n + 1) * BLOCK, :]
    body[...] = total
    for p in range(8):
        piece = body[SIDE : SIDE + 16, :]
        last[p * 16 : p * 16 + 16, :] = piece if p == 0 else pltpu.roll(piece, (LANES - p * 16) % LANES, 1)
    last[128:144, :] = body[SIDE + 16 : BLOCK, :]
    lane = lax.broadcasted_iota(jnp.int32, (9, LANES), 1)
    grads = jnp.zeros((9, LANES), F32)
    for q in range(9):
        halves = [jnp.zeros((9, LANES), F32), jnp.zeros((9, LANES), F32)]
        diag = jnp.zeros((9, LANES), F32)
        for c in range(CAM_ROW):
            ref, at = (body, q * 16) if q < 8 else (last, 0)
            x = ref[pl.ds(c, 9, stride=16), :]
            turn = pltpu.roll(x, (c * NBR - at) % LANES, 1)
            for half in range(2):
                lo, hi = c * NBR - half * LANES, (c + 1) * NBR - half * LANES
                if hi > 0 and lo < LANES:
                    halves[half] = jnp.where((lane >= lo) & (lane < hi), turn, halves[half])
            diag = jnp.where(lane == c, pltpu.roll(x, (c - at - 14) % LANES, 1), diag)
            if q == 0:
                grads = jnp.where(lane == c, pltpu.roll(x, (c - at - 15) % LANES, 1), grads)
        for n, x in enumerate((halves[0], halves[1], diag)):
            rows[pl.ds(n * 88 + q, 9, stride=9), :] = x
    pair[:, 0:LANES] = rows[0:81, :]
    pair[:, LANES : CAM_ROW * NBR] = rows[88:169, : CAM_ROW * NBR - LANES]
    hess[...] = rows[176:257, :CAM_ROW]
    grad[...] = grads[:, :CAM_ROW]


def on_device(
    camera_jacobian, point_jacobian, residual, send_order, camera_of, track_of, partner, pair_slot
):
    peers = lax.axis_size("obs")
    msg, own = pl.pallas_call(
        pack_kernel,
        out_shape=(
            jax.ShapeDtypeStruct((peers * ROWS_IN, LANES), F32),
            jax.ShapeDtypeStruct((32, SLOTS), F32),
        ),
        scratch_shapes=[pltpu.VMEM((32, SLOTS), F32)],
        name="pack",
    )(camera_jacobian, point_jacobian, residual, camera_of.reshape(1, SLOTS), send_order.reshape(1, SLOTS))
    owned = lax.all_to_all(msg.reshape(peers, ROWS_IN, LANES), "obs", 0, 0, tiled=True)
    returned = pl.pallas_call(
        owner_kernel,
        out_shape=jax.ShapeDtypeStruct((peers * ROWS_BACK, LANES), F32),
        scratch_shapes=[
            pltpu.VMEM((RANKS * 8, LANES), jnp.int32),
            pltpu.VMEM((5 * 26, 8, LANES), F32),
            pltpu.VMEM((RANKS * 6, 8, LANES), F32),
            pltpu.VMEM((132, 8, LANES), F32),
        ],
        name="owner",
    )(owned.reshape(peers * ROWS_IN, LANES), partner)
    back = lax.all_to_all(returned.reshape(peers, ROWS_BACK, LANES), "obs", 0, 0, tiled=True)
    blocks = pl.pallas_call(
        camera_kernel,
        out_shape=jax.ShapeDtypeStruct((8 * BLOCK, LANES), F32),
        scratch_shapes=[
            pltpu.VMEM((SIDE, 2 * SLOTS), BF16),
            pltpu.VMEM((SIDE, 2 * SLOTS), BF16),
            pltpu.VMEM((SIDE, 2 * SLOTS), BF16),
            pltpu.VMEM((SIDE, 2 * SLOTS), BF16),
            pltpu.VMEM((SIDE, LANES), F32),
            pltpu.VMEM((4 * ROWS_BACK, LANES), F32),
        ],
        name="camera",
    )(back.reshape(peers * ROWS_BACK, LANES), own, pair_slot)
    parts = lax.all_to_all(blocks.reshape(8, BLOCK, LANES), "row", 0, 0, tiled=True)
    return pl.pallas_call(
        final_kernel,
        out_shape=(
            jax.ShapeDtypeStruct((81, CAM_ROW), F32),
            jax.ShapeDtypeStruct((9, CAM_ROW), F32),
            jax.ShapeDtypeStruct((81, CAM_ROW * NBR), F32),
        ),
        scratch_shapes=[pltpu.VMEM((BLOCK, LANES), F32), pltpu.VMEM((SIDE, LANES), F32), pltpu.VMEM((264, LANES), F32)],
        name="final",
    )(parts.reshape(8 * BLOCK, LANES))


def solution(mesh):
    return jax.shard_map(
        on_device,
        mesh=mesh,
        in_specs=(
            P(None, ("obs", "row")),
            P(None, ("obs", "row")),
            P(None, ("obs", "row")),
            P(("obs", "row")),
            P(("obs", "row")),
            P(("obs", "row")),
            P(None, ("obs", "row")),
            P(None, ("obs", "row")),
        ),
        out_specs=(P(None, ("obs", "row")), P(None, ("obs", "row")), P(None, ("obs", "row"))),
        check_vma=False,
    )
```

time: 269 us -> 95.4 us (0.35); the launches traced: 264 us -> 95 us
  waiting for transfers between devices: 87.8 us -> 0 us
  local copies, waits for them, and re-layouts: 81.8 us -> 1.46 us
  blocking collectives: 0 us -> 64.5 us
  other arithmetic: 58.4 us -> 0 us
  Pallas kernels: 0 us -> 28.3 us
  starting transfers between devices: 20.3 us -> 0 us
  between operations: 14.7 us -> 0.64 us
    all_to_all x0 -> x3, blocking collectives: none -> 64.5 us  [the longest x1 30.5 us: on_device(): lax.all_to_all(blocks.reshape(8, BLOCK, LANES), 'row', 0, 0, tiled=True)]
    all_to_all x3 -> x0, waiting for transfers between devices: 53.2 us -> none  [the longest x1 47.1 us: on_device(): lax.all_to_all(block_values.reshape(81, ranks, obs_count), 'obs', split_a...]
    scatter-add x2 -> x0, other arithmetic: 46.6 us -> none  [the longest x1 40.5 us: on_device(): jnp.zeros((81, slot_count + 1), jnp.float32).at[:, pair_slot.reshape(-1)]]
    gather x6 -> x0, local copies, waits for them, and re-layouts: 34.7 us -> none  [the longest x1 24.2 us: on_device(): chosen = jnp.take(flat_factor, partner.reshape(-1), axis=1)]
    reduce_scatter x2 -> x0, waiting for transfers between devices: 34.6 us -> none  [the longest x1 34.5 us: on_device(): lax.psum_scatter(pair_total[:, :slot_count], 'row', scatter_dimension=1,...]
    pallas_call x0 -> x4, Pallas kernels: none -> 28.3 us  [the longest x1 15.8 us: on_device(): pl.pallas_call(camera_kernel, out_shape=jax.ShapeDtypeStruct((8 * BLOCK,...]
    all_to_all x3 -> x0, starting transfers between devices: 20 us -> none  [the longest x1 8.58 us: on_device(): owned = lax.all_to_all(sent, 'obs', split_axis=1, concat_axis=1, tiled=True)]
    mul x22 -> x0, local copies, waits for them, and re-layouts: 12.7 us -> none  [the longest x3 4.24 us: pair_product(): left[0][:, None] * right[0][None, :] + left[1][:, None] * right[1][None, :]]
  transfers between devices with their start and end apart: 5 -> 0, of which waited for: 3 -> 0; matrix products, arithmetic and copies ran while one was open for 41% -> 0% of each run, Pallas kernels for 0% -> 0%
where the time goes in v1:
time: 95.4 us; the launch traced here: 95 us
  blocking collectives  64.5 us (68%)
  Pallas kernels  28.3 us (30%)
  local copies, waits for them, and re-layouts  1.46 us (2%)
    all_to_all x1, blocking collectives, on_device(): lax.all_to_all(blocks.reshape(8, BLOCK, LANES), 'row', 0, 0, tiled=True)  30.5 us
    all_to_all x1, blocking collectives, on_device(): lax.all_to_all(returned.reshape(peers, ROWS_BACK, LANES), 'obs', 0, 0, ti...  17.7 us
    all_to_all x1, blocking collectives, on_device(): lax.all_to_all(msg.reshape(peers, ROWS_IN, LANES), 'obs', 0, 0, tiled=True)  16.4 us
    pallas_call x1, Pallas kernels, on_device(): pl.pallas_call(camera_kernel, out_shape=jax.ShapeDtypeStruct((8 * BLOCK,...  15.8 us
    pallas_call x1, Pallas kernels, on_device(): pl.pallas_call(owner_kernel, out_shape=jax.ShapeDtypeStruct((peers * ROWS...  7 us
    pallas_call x1, Pallas kernels, on_device(): pl.pallas_call(pack_kernel, out_shape=(jax.ShapeDtypeStruct((peers * ROWS...  3.09 us
    pallas_call x1, Pallas kernels, on_device(): pl.pallas_call(final_kernel, out_shape=(jax.ShapeDtypeStruct((81, CAM_ROW...  2.5 us

profile of v1, /device:TPU:1, one launch (start us, length us, event | category | flops | bytes accessed | tf_op | source)
XLA Modules:
  0.0 95.0 jit_solution(13011004649444182723)
XLA Ops:
  0.6 3.1 %pack.1 = (f32[256,128]{1,0:T(8,128)}, f32[32,1024]{1,0:T(8,128)}) custom-call(f32[18,1024]{1,0:T(8,128)} %jc.1, f32[6,1024]{1,0:T(8,128)} %jp.1, f32[2,1024]{1,0:T(2,128)} %err.1, s32[1,1024]{1,0:T(1,128)} %bitcast.14, s32[1,1024]{1,0:T(1,128)} %bitcast.15), custom_call_target="tpu_custom_call" | custom-call | tf_op jit(solution)/shard_map/pack/pallas_call | solution.py:289
  3.7 16.4 %all_to_all.15 = f32[32,8,128]{2,1,0:T(8,128)} all-to-all(f32[32,8,128]{2,1,0:T(8,128)} %bitcast.13), channel_id=1, replica_groups=mesh['obs'=32,'row'=8] {'obs'}, dimensions={0} | all-to-all | bytes 262144 | tf_op jit(solution)/shard_map/all_to_all | solution.py:298
  20.1 7.0 %owner.1 = f32[1280,128]{1,0:T(8,128)} custom-call(f32[256,128]{1,0:T(8,128)} %bitcast.12, s32[7,1024]{1,0:T(8,128)} %partner.1), custom_call_target="tpu_custom_call" | custom-call | tf_op jit(solution)/shard_map/owner/pallas_call | solution.py:299
  27.1 17.7 %all_to_all.16 = f32[32,40,128]{2,1,0:T(8,128)} all-to-all(f32[32,40,128]{2,1,0:T(8,128)} %bitcast.11), channel_id=1, replica_groups=mesh['obs'=32,'row'=8] {'obs'}, dimensions={0} | all-to-all | bytes 1310720 | tf_op jit(solution)/shard_map/all_to_all | solution.py:310
  44.7 15.8 %camera.1 = f32[1408,128]{1,0:T(8,128)} custom-call(f32[1280,128]{1,0:T(8,128)} %bitcast.10, f32[32,1024]{1,0:T(8,128)} %get-tuple-element.6.own, s32[7,1024]{1,0:T(8,128)} %pair_slot.1), custom_call_target="tpu_custom_call" | custom-call | tf_op jit(solution)/shard_map/camera/pallas_call | solution.py:311
  60.5 30.5 %all_to_all.17 = f32[8,176,128]{2,1,0:T(8,128)} all-to-all(f32[8,176,128]{2,1,0:T(8,128)} %bitcast.9), channel_id=1, replica_groups=mesh['obs'=32,'row'=8] {'row'}, dimensions={0} | all-to-all | bytes 1441792 | tf_op jit(solution)/shard_map/all_to_all | solution.py:324
  91.0 2.5 %final.1 = (f32[81,16]{1,0:T(8,128)}, f32[9,16]{1,0:T(8,128)}, f32[81,224]{1,0:T(8,128)}) custom-call(f32[1408,128]{1,0:T(8,128)} %bitcast.8), custom_call_target="tpu_custom_call" | custom-call | tf_op jit(solution)/shard_map/final/pallas_call | solution.py:325
  93.5 1.5 %copy.10 = f32[81,16]{0,1:T(8,128)} copy(f32[81,16]{1,0:T(8,128)} %get-tuple-element.7) | data formatting | bytes 10368 | tf_op jit(solution)/shard_map/final/pallas_call | solution.py:325

commit v2 on v1

--- a/solution.py
+++ b/solution.py
@@ -1,3 +1,5 @@
+import functools
+
 import jax
 import jax.numpy as jnp
 from jax import lax
@@ -18,6 +20,7 @@
 SIDE = 144
 BLOCK = 176
 damping = 1.0
+COST = pl.CostEstimate(flops=4_000_000_000, bytes_accessed=4_000_000, transcendentals=0)
 F32 = jnp.float32
 BF16 = jnp.bfloat16
 
@@ -211,7 +214,7 @@
     return lax.dot_general(x, y, (((1,), (1,)), ((), ())), preferred_element_type=F32)
 
 
-def build_block(dest, own, right_hi, right_lo, left_hi, left_lo, wide, out, base):
+def build_block(dest, own, right_hi, right_lo, left_hi, left_lo, wide, out):
     low = lax.broadcasted_iota(jnp.int32, (16, LANES), 0).astype(F32) + (dest * CAM_ROW).astype(F32)
 
     def chunk(d, _):
@@ -232,28 +235,31 @@
     total = dot_t(left_hi[...], right_hi[...]) + (
         dot_t(left_hi[...], right_lo[...]) + dot_t(left_lo[...], right_hi[...])
     )
-    out[base : base + SIDE, :] = total[:, :LANES]
+    out[0:SIDE, :] = total[:, :LANES]
     wide[:, 0:16] = total[:, LANES:]
     lane = lax.broadcasted_iota(jnp.int32, (16, LANES), 1)
     tail = wide[0:16, :]
     for p in range(1, 8):
         tail = jnp.where(lane // 16 == p, pltpu.roll(wide[p * 16 : p * 16 + 16, :], p * 16, 1), tail)
-    out[base + SIDE : base + SIDE + 16, :] = tail
-    out[base + SIDE + 16 : base + BLOCK, :] = wide[128:144, :]
-
-
-def camera_kernel(back, own, pair_slot, out, right_hi, right_lo, left_hi, left_lo, wide, flat):
+    out[SIDE : SIDE + 16, :] = tail
+    out[SIDE + 16 : BLOCK, :] = wide[128:144, :]
+
+
+def first_kernel(row, back, own, pair_slot, plus, minus, right_hi, right_lo, left_hi, left_lo, wide, flat):
     build_right(back, own, pair_slot, right_hi, right_lo, flat)
     wide[...] = jnp.zeros((SIDE, LANES), F32)
-    for dest in range(8):
-        build_block(jnp.int32(dest), own, right_hi, right_lo, left_hi, left_lo, wide, out, dest * BLOCK)
-
-
-def final_kernel(parts, hess, grad, pair, body, last, rows):
-    total = parts[0:BLOCK, :]
-    for n in range(1, 8):
-        total = total + parts[n * BLOCK : (n + 1) * BLOCK, :]
-    body[...] = total
+    build_block((row[0] + 4) % 8, own, right_hi, right_lo, left_hi, left_lo, wide, plus)
+    build_block((row[0] + 5) % 8, own, right_hi, right_lo, left_hi, left_lo, wide, minus)
+
+
+def next_kernel(step, row, own, right_hi, right_lo, plus, minus, left_hi, left_lo, wide):
+    wide[...] = jnp.zeros((SIDE, LANES), F32)
+    build_block((row[0] + 4 - step) % 8, own, right_hi, right_lo, left_hi, left_lo, wide, plus)
+    build_block((row[0] + 5 + step) % 8, own, right_hi, right_lo, left_hi, left_lo, wide, minus)
+
+
+def final_kernel(own, plus, minus, hess, grad, pair, body, last, rows):
+    body[...] = own[...] + (plus[...] + minus[...])
     for p in range(8):
         piece = body[SIDE : SIDE + 16, :]
         last[p * 16 : p * 16 + 16, :] = piece if p == 0 else pltpu.roll(piece, (LANES - p * 16) % LANES, 1)
@@ -262,7 +268,6 @@
     grads = jnp.zeros((9, LANES), F32)
     for q in range(9):
         halves = [jnp.zeros((9, LANES), F32), jnp.zeros((9, LANES), F32)]
-        diag = jnp.zeros((9, LANES), F32)
         for c in range(CAM_ROW):
             ref, at = (body, q * 16) if q < 8 else (last, 0)
             x = ref[pl.ds(c, 9, stride=16), :]
@@ -271,14 +276,20 @@
                 lo, hi = c * NBR - half * LANES, (c + 1) * NBR - half * LANES
                 if hi > 0 and lo < LANES:
                     halves[half] = jnp.where((lane >= lo) & (lane < hi), turn, halves[half])
-            diag = jnp.where(lane == c, pltpu.roll(x, (c - at - 14) % LANES, 1), diag)
             if q == 0:
                 grads = jnp.where(lane == c, pltpu.roll(x, (c - at - 15) % LANES, 1), grads)
-        for n, x in enumerate((halves[0], halves[1], diag)):
+        for n, x in enumerate(halves):
             rows[pl.ds(n * 88 + q, 9, stride=9), :] = x
     pair[:, 0:LANES] = rows[0:81, :]
     pair[:, LANES : CAM_ROW * NBR] = rows[88:169, : CAM_ROW * NBR - LANES]
-    hess[...] = rows[176:257, :CAM_ROW]
+    lane = lax.broadcasted_iota(jnp.int32, (16, LANES), 1)
+    diag = jnp.zeros((16, LANES), F32)
+    for p in range(9):
+        for q in range(9):
+            ref, at = (body, q * 16) if q < 8 else (last, 0)
+            x = ref[p * 16 : p * 16 + 16, :]
+            diag = jnp.where(lane == p * 9 + q, pltpu.roll(x, (p * 9 + q - at - 14) % LANES, 1), diag)
+    hess[...] = diag[:, :81]
     grad[...] = grads[:, :CAM_ROW]
 
 
@@ -308,30 +319,54 @@
         name="owner",
     )(owned.reshape(peers * ROWS_IN, LANES), partner)
     back = lax.all_to_all(returned.reshape(peers, ROWS_BACK, LANES), "obs", 0, 0, tiled=True)
-    blocks = pl.pallas_call(
-        camera_kernel,
-        out_shape=jax.ShapeDtypeStruct((8 * BLOCK, LANES), F32),
-        scratch_shapes=[
-            pltpu.VMEM((SIDE, 2 * SLOTS), BF16),
-            pltpu.VMEM((SIDE, 2 * SLOTS), BF16),
-            pltpu.VMEM((SIDE, 2 * SLOTS), BF16),
-            pltpu.VMEM((SIDE, 2 * SLOTS), BF16),
-            pltpu.VMEM((SIDE, LANES), F32),
-            pltpu.VMEM((4 * ROWS_BACK, LANES), F32),
-        ],
-        name="camera",
-    )(back.reshape(peers * ROWS_BACK, LANES), own, pair_slot)
-    parts = lax.all_to_all(blocks.reshape(8, BLOCK, LANES), "row", 0, 0, tiled=True)
-    return pl.pallas_call(
+    row = lax.axis_index("row").astype(jnp.int32).reshape(1)
+    here = pl.BlockSpec(memory_space=pltpu.VMEM)
+    scalar = pl.BlockSpec(memory_space=pltpu.SMEM)
+    block = jax.ShapeDtypeStruct((BLOCK, LANES), F32)
+    side = jax.ShapeDtypeStruct((SIDE, 2 * SLOTS), BF16)
+    left = [pltpu.VMEM((SIDE, 2 * SLOTS), BF16), pltpu.VMEM((SIDE, 2 * SLOTS), BF16), pltpu.VMEM((SIDE, LANES), F32)]
+    params = pltpu.CompilerParams(vmem_limit_bytes=16 << 20)
+    plus, minus, right_hi, right_lo = pl.pallas_call(
+        first_kernel,
+        in_specs=[scalar, here, here, here],
+        out_shape=(block, block, side, side),
+        scratch_shapes=left + [pltpu.VMEM((4 * ROWS_BACK, LANES), F32)],
+        compiler_params=params,
+        cost_estimate=COST,
+        name="camera_0",
+    )(row, back.reshape(peers * ROWS_BACK, LANES), own, pair_slot)
+    for step in range(1, 4):
+        plus = lax.ppermute(plus, "row", [(n, (n + 1) % 8) for n in range(8)])
+        minus = lax.ppermute(minus, "row", [(n, (n - 1) % 8) for n in range(8)])
+        more_plus, more_minus = pl.pallas_call(
+            functools.partial(next_kernel, step),
+            in_specs=[scalar, here, here, here],
+            out_shape=(block, block),
+            scratch_shapes=left,
+            compiler_params=params,
+            cost_estimate=COST,
+            name=f"camera_{step}",
+        )(row, own, right_hi, right_lo)
+        plus = plus + more_plus
+        if step < 3:
+            minus = minus + more_minus
+    plus = lax.ppermute(plus, "row", [(n, (n + 1) % 8) for n in range(8)])
+    hess, grad, pair = pl.pallas_call(
         final_kernel,
         out_shape=(
-            jax.ShapeDtypeStruct((81, CAM_ROW), F32),
+            jax.ShapeDtypeStruct((CAM_ROW, 81), F32),
             jax.ShapeDtypeStruct((9, CAM_ROW), F32),
             jax.ShapeDtypeStruct((81, CAM_ROW * NBR), F32),
         ),
-        scratch_shapes=[pltpu.VMEM((BLOCK, LANES), F32), pltpu.VMEM((SIDE, LANES), F32), pltpu.VMEM((264, LANES), F32)],
+        scratch_shapes=[
+            pltpu.VMEM((BLOCK, LANES), F32),
+            pltpu.VMEM((SIDE, LANES), F32),
+            pltpu.VMEM((176, LANES), F32),
+        ],
+        compiler_params=params,
         name="final",
-    )(parts.reshape(8 * BLOCK, LANES))
+    )(more_minus, plus, minus)
+    return hess.T, grad, pair
 
 
 def solution(mesh):

time: 95.4 us -> 75.7 us (0.79)
  blocking collectives: 64.5 us -> 16.4 us
  waiting for transfers between devices: 0 us -> 17.7 us
  starting transfers between devices: 0 us -> 15.5 us
  Pallas kernels: 28.3 us -> 25 us
  local copies, waits for them, and re-layouts: 1.46 us -> 0.01 us
    all_to_all x2 -> x0, blocking collectives: 48.2 us -> none  [the longest x1 30.5 us: on_device(): lax.all_to_all(blocks.reshape(8, BLOCK, LANES), 'row', 0, 0, tiled=True)]
    all_to_all x0 -> x1, waiting for transfers between devices: none -> 13 us  [on_device(): lax.all_to_all(returned.reshape(peers, ROWS_BACK, LANES), 'obs', 0, 0, ti...]
    ppermute x0 -> x7, starting transfers between devices: none -> 11.5 us  [the longest x3 9.5 us: on_device(): minus = lax.ppermute(minus, 'row', [(n, (n - 1) % 8) for n in range(8)])]
    ppermute x0 -> x7, waiting for transfers between devices: none -> 4.66 us  [the longest x4 3.2 us: on_device(): plus = lax.ppermute(plus, 'row', [(n, (n + 1) % 8) for n in range(8)])]
    all_to_all x0 -> x1, starting transfers between devices: none -> 4.08 us  [on_device(): lax.all_to_all(returned.reshape(peers, ROWS_BACK, LANES), 'obs', 0, 0, ti...]
    pallas_call x2 -> x5, Pallas kernels: 18.3 us -> 14.9 us  [the longest x3 9.05 us: on_device(): pl.pallas_call(functools.partial(next_kernel, step), in_specs=[scalar, he...]
    pallas_call x1 -> x0, local copies, waits for them, and re-layouts: 1.46 us -> none  [on_device(): pl.pallas_call(final_kernel, out_shape=(jax.ShapeDtypeStruct((81, CAM_ROW...]
  transfers between devices with their start and end apart: 0 -> 8, of which waited for: 0 -> 4; matrix products, arithmetic and copies ran while one was open for 0% -> 0% of each run, Pallas kernels for 0% -> 12%
where the time goes in v2:
time: 75.7 us; the launch traced here: 75.4 us
  Pallas kernels  25 us (33%)
  waiting for transfers between devices  17.7 us (23%)
  blocking collectives  16.4 us (22%)
  starting transfers between devices  15.5 us (20%)
    all_to_all x1, blocking collectives, on_device(): lax.all_to_all(msg.reshape(peers, ROWS_IN, LANES), 'obs', 0, 0, tiled=True)  16.4 us
    all_to_all x1, waiting for transfers between devices, on_device(): lax.all_to_all(returned.reshape(peers, ROWS_BACK, LANES), 'obs', 0, 0, ti...  13 us
    ppermute x3, starting transfers between devices, on_device(): minus = lax.ppermute(minus, 'row', [(n, (n - 1) % 8) for n in range(8)])  9.5 us
    pallas_call x3, Pallas kernels, on_device(): pl.pallas_call(functools.partial(next_kernel, step), in_specs=[scalar, he...  9.05 us
    pallas_call x1, Pallas kernels, on_device(): pl.pallas_call(owner_kernel, out_shape=jax.ShapeDtypeStruct((peers * ROWS...  7 us
    pallas_call x1, Pallas kernels, on_device(): pl.pallas_call(first_kernel, in_specs=[scalar, here, here, here], out_sha...  4.63 us
    all_to_all x1, starting transfers between devices, on_device(): lax.all_to_all(returned.reshape(peers, ROWS_BACK, LANES), 'obs', 0, 0, ti...  4.08 us
    ppermute x4, waiting for transfers between devices, on_device(): plus = lax.ppermute(plus, 'row', [(n, (n + 1) % 8) for n in range(8)])  3.2 us
  transfers between devices with their start and end apart: 8, of which 4 were waited for; matrix products, arithmetic and copies ran while one was open for 0% of the time, Pallas kernels for 12%

profile of v2, /device:TPU:1, one launch (start us, length us, event | category | flops | bytes accessed | tf_op | source)
XLA Modules:
  0.0 75.4 jit_solution(3738009588661157068)
XLA Ops:
  0.6 3.1 %pack.1 = (f32[256,128]{1,0:T(8,128)}, f32[32,1024]{1,0:T(8,128)}) custom-call(f32[18,1024]{1,0:T(8,128)} %jc.1, f32[6,1024]{1,0:T(8,128)} %jp.1, f32[2,1024]{1,0:T(2,128)} %err.1, s32[1,1024]{1,0:T(1,128)} %bitcast.12, s32[1,1024]{1,0:T(1,128)} %bitcast.13), custom_call_target="tpu_custom_call" | custom-call | tf_op jit(solution)/shard_map/pack/pallas_call | solution.py:300
  3.7 16.4 %all_to_all.10 = f32[32,8,128]{2,1,0:T(8,128)} all-to-all(f32[32,8,128]{2,1,0:T(8,128)} %bitcast.11), channel_id=1, replica_groups=mesh['obs'=32,'row'=8] {'obs'}, dimensions={0} | all-to-all | bytes 262144 | tf_op jit(solution)/shard_map/all_to_all | solution.py:309
  20.1 7.0 %owner.1 = f32[1280,128]{1,0:T(8,128)} custom-call(f32[256,128]{1,0:T(8,128)} %bitcast.10, s32[7,1024]{1,0:T(8,128)} %partner.1), custom_call_target="tpu_custom_call" | custom-call | tf_op jit(solution)/shard_map/owner/pallas_call | solution.py:310
  27.1 0.0 copy-start
  27.1 0.0 copy-start.1
  27.1 4.1 %all-to-all-start.1 = ((f32[32,40,128]{2,1,0:T(8,128)}), f32[32,40,128]{2,1,0:T(8,128)S(1)}, u32[]{:S(2)}, u32[]{:S(2)}) async-start(f32[32,40,128]{2,1,0:T(8,128)} %bitcast.9), calls=%async_computation.1 | async-start | bytes 1310720 | tf_op jit(solution)/shard_map/all_to_all | solution.py:321
  31.2 13.0 %all-to-all-done.1 = f32[32,40,128]{2,1,0:T(8,128)S(1)} async-done(((f32[32,40,128]{2,1,0:T(8,128)}), f32[32,40,128]{2,1,0:T(8,128)S(1)}, u32[]{:S(2)}, u32[]{:S(2)}) %all-to-all-start.1) | async-done | bytes 655392 | tf_op jit(solution)/shard_map/all_to_all | solution.py:321
  44.2 0.0 copy-done
  44.2 0.0 copy-done.1
  44.2 4.6 %camera_0.1 = (f32[176,128]{1,0:T(8,128)S(1)}, f32[176,128]{1,0:T(8,128)S(1)}, bf16[144,2048]{1,0:T(8,128)(2,1)S(1)}, bf16[144,2048]{1,0:T(8,128)(2,1)S(1)}) custom-call(s32[1]{0:T(128)} %bitcast.row, f32[1280,128]{1,0:T(8,128)S(1)} %bitcast.8, f32[32,1024]{1,0:T(8,128)S(1)} %copy-done, s32[7,1024]{1,0:T(8,128)S(1)} %copy-done.1), custom_call_target="tpu_custom_call" | custom-call | flops 4000000000 | bytes 4000000 | tf_op jit(solution)/shard_map/camera_0/pallas_call | solution.py:329
  48.9 1.7 %collective-permute-start = (f32[176,128]{1,0:T(8,128)S(1)}, f32[176,128]{1,0:T(8,128)S(1)}, u32[]{:S(2)}, u32[]{:S(2)}) collective-permute-start(f32[176,128]{1,0:T(8,128)S(1)} %get-tuple-element.23), channel_id=1, source_target_pairs={{0,1},{1,2},{2,3},{3,4},{4,5},{5,6},{6,7},{7,0},{8,9},{9,10},{10,1... | collective-permute-start | bytes 270344 | tf_op jit(solution)/shard_map/ppermute | solution.py:339
  50.6 4.0 %collective-permute-start.4 = (f32[176,128]{1,0:T(8,128)S(1)}, f32[176,128]{1,0:T(8,128)S(1)}, u32[]{:S(2)}, u32[]{:S(2)}) collective-permute-start(f32[176,128]{1,0:T(8,128)S(1)} %get-tuple-element.27), channel_id=1, source_target_pairs={{0,7},{1,0},{2,1},{3,2},{4,3},{5,4},{6,5},{7,6},{8,15},{9,8},{10,9... | collective-permute-start | bytes 270344 | tf_op jit(solution)/shard_map/ppermute | solution.py:340
  54.6 3.0 %camera_1.1 = (f32[176,128]{1,0:T(8,128)S(1)}, f32[176,128]{1,0:T(8,128)S(1)}) custom-call(s32[1]{0:T(128)} %bitcast.row, f32[32,1024]{1,0:T(8,128)S(1)} %copy-done, bf16[144,2048]{1,0:T(8,128)(2,1)S(1)} %get-tuple-element.20.right_hi, bf16[144,2048]{1,0:T(8,128)(2,1)S(1)} %get-tuple-element.21.right_lo), custom_call_target="tpu_custom_call" | custom-call | flops 4000000000 | bytes 4000000 | tf_op jit(solution)/shard_map/camera_1/pallas_call | solution.py:341
  57.6 0.1 collective-permute-done
  57.7 0.1 collective-permute-start.1
  57.8 3.0 %camera_2.1 = (f32[176,128]{1,0:T(8,128)S(1)}, f32[176,128]{1,0:T(8,128)S(1)}) custom-call(s32[1]{0:T(128)} %bitcast.row, f32[32,1024]{1,0:T(8,128)S(1)} %copy-done, bf16[144,2048]{1,0:T(8,128)(2,1)S(1)} %get-tuple-element.20.right_hi, bf16[144,2048]{1,0:T(8,128)(2,1)S(1)} %get-tuple-element.21.right_lo), custom_call_target="tpu_custom_call" | custom-call | flops 4000000000 | bytes 4000000 | tf_op jit(solution)/shard_map/camera_2/pallas_call | solution.py:341
  60.8 0.0 collective-permute-done.4
  60.8 2.7 %collective-permute-start.5 = (f32[176,128]{1,0:T(8,128)S(1)}, f32[176,128]{1,0:T(8,128)S(1)}, u32[]{:S(2)}, u32[]{:S(2)}) collective-permute-start(f32[176,128]{1,0:T(8,128)S(1)} %add.18), channel_id=1, source_target_pairs={{0,7},{1,0},{2,1},{3,2},{4,3},{5,4},{6,5},{7,6},{8,15},{9,8},{10,9... | collective-permute-start | bytes 270344 | tf_op jit(solution)/shard_map/ppermute | solution.py:340
  63.6 0.0 collective-permute-done.1
  63.6 0.1 collective-permute-start.2
  63.7 3.0 %camera_3.1 = (f32[176,128]{1,0:T(8,128)S(1)}, f32[176,128]{1,0:T(8,128)S(1)}) custom-call(s32[1]{0:T(128)} %bitcast.row, f32[32,1024]{1,0:T(8,128)S(1)} %copy-done, bf16[144,2048]{1,0:T(8,128)(2,1)S(1)} %get-tuple-element.20.right_hi, bf16[144,2048]{1,0:T(8,128)(2,1)S(1)} %get-tuple-element.21.right_lo), custom_call_target="tpu_custom_call" | custom-call | flops 4000000000 | bytes 4000000 | tf_op jit(solution)/shard_map/camera_3/pallas_call | solution.py:341
  66.7 0.0 collective-permute-done.5
  66.7 2.7 %collective-permute-start.6 = (f32[176,128]{1,0:T(8,128)S(1)}, f32[176,128]{1,0:T(8,128)S(1)}, u32[]{:S(2)}, u32[]{:S(2)}) collective-permute-start(f32[176,128]{1,0:T(8,128)S(1)} %add.19), channel_id=1, source_target_pairs={{0,7},{1,0},{2,1},{3,2},{4,3},{5,4},{6,5},{7,6},{8,15},{9,8},{10,9... | collective-permute-start | bytes 270344 | tf_op jit(solution)/shard_map/ppermute | solution.py:340
  69.5 0.0 collective-permute-done.2
  69.5 0.1 collective-permute-start.3
  69.6 1.5 %collective-permute-done.6.minus = f32[176,128]{1,0:T(8,128)S(1)} collective-permute-done((f32[176,128]{1,0:T(8,128)S(1)}, f32[176,128]{1,0:T(8,128)S(1)}, u32[]{:S(2)}, u32[]{:S(2)}) %collective-permute-start.6) | collective-permute-done | bytes 90144 | tf_op jit(solution)/shard_map/ppermute | solution.py:340
  71.0 3.1 %collective-permute-done.3.plus = f32[176,128]{1,0:T(8,128)S(1)} collective-permute-done((f32[176,128]{1,0:T(8,128)S(1)}, f32[176,128]{1,0:T(8,128)S(1)}, u32[]{:S(2)}, u32[]{:S(2)}) %collective-permute-start.3) | collective-permute-done | bytes 90144 | tf_op jit(solution)/shard_map/ppermute | solution.py:353
  74.2 1.2 %final.1 = (f32[16,81]{1,0:T(8,128)}, f32[9,16]{1,0:T(8,128)}, f32[81,224]{1,0:T(8,128)}) custom-call(f32[176,128]{1,0:T(8,128)S(1)} %get-tuple-element.22.own, f32[176,128]{1,0:T(8,128)S(1)} %collective-permute-done.3.plus, f32[176,128]{1,0:T(8,128)S(1)} %collective-permute-done.6.minus), custom_call_target="tpu_custom_call" | custom-call | tf_op jit(solution)/shard_map/final/pallas_call | solution.py:354
  (5 shorter events, 0.1 us)
Async XLA Ops:
  27.1 17.1 %copy-start = (f32[32,1024]{1,0:T(8,128)S(1)}, f32[32,1024]{1,0:T(8,128)}, u32[]{:S(2)}) copy-start(f32[32,1024]{1,0:T(8,128)} %get-tuple-element.18.own) | copy-start | bytes 393220
  27.1 17.1 %copy-start.1 = (s32[7,1024]{1,0:T(8,128)S(1)}, s32[7,1024]{1,0:T(8,128)}, u32[]{:S(2)}) copy-start(s32[7,1024]{1,0:T(8,128)} %pair_slot.1) | copy-start | bytes 86020
  27.1 17.1 %all-to-all-start.1 = ((f32[32,40,128]{2,1,0:T(8,128)}), f32[32,40,128]{2,1,0:T(8,128)S(1)}, u32[]{:S(2)}, u32[]{:S(2)}) async-start(f32[32,40,128]{2,1,0:T(8,128)} %bitcast.9), calls=%async_computation.1 | async-start | bytes 1310720 | tf_op jit(solution)/shard_map/all_to_all | solution.py:321
  48.9 8.8 %collective-permute-start = (f32[176,128]{1,0:T(8,128)S(1)}, f32[176,128]{1,0:T(8,128)S(1)}, u32[]{:S(2)}, u32[]{:S(2)}) collective-permute-start(f32[176,128]{1,0:T(8,128)S(1)} %get-tuple-element.23), channel_id=1, source_target_pairs={{0,1},{1,2},{2,3},{3,4},{4,5},{5,6},{6,7},{7,0},{8,9},{9,10},{10,1... | collective-permute-start | bytes 270344 | tf_op jit(solution)/shard_map/ppermute | solution.py:339
  50.6 10.2 %collective-permute-start.4 = (f32[176,128]{1,0:T(8,128)S(1)}, f32[176,128]{1,0:T(8,128)S(1)}, u32[]{:S(2)}, u32[]{:S(2)}) collective-permute-start(f32[176,128]{1,0:T(8,128)S(1)} %get-tuple-element.27), channel_id=1, source_target_pairs={{0,7},{1,0},{2,1},{3,2},{4,3},{5,4},{6,5},{7,6},{8,15},{9,8},{10,9... | collective-permute-start | bytes 270344 | tf_op jit(solution)/shard_map/ppermute | solution.py:340
  57.7 5.9 %collective-permute-start.1 = (f32[176,128]{1,0:T(8,128)S(1)}, f32[176,128]{1,0:T(8,128)S(1)}, u32[]{:S(2)}, u32[]{:S(2)}) collective-permute-start(f32[176,128]{1,0:T(8,128)S(1)} %add.15), channel_id=1, source_target_pairs={{0,1},{1,2},{2,3},{3,4},{4,5},{5,6},{6,7},{7,0},{8,9},{9,10},{10,1... | collective-permute-start | bytes 270344 | tf_op jit(solution)/shard_map/ppermute | solution.py:339
  60.8 5.9 %collective-permute-start.5 = (f32[176,128]{1,0:T(8,128)S(1)}, f32[176,128]{1,0:T(8,128)S(1)}, u32[]{:S(2)}, u32[]{:S(2)}) collective-permute-start(f32[176,128]{1,0:T(8,128)S(1)} %add.18), channel_id=1, source_target_pairs={{0,7},{1,0},{2,1},{3,2},{4,3},{5,4},{6,5},{7,6},{8,15},{9,8},{10,9... | collective-permute-start | bytes 270344 | tf_op jit(solution)/shard_map/ppermute | solution.py:340
  63.6 5.9 %collective-permute-start.2 = (f32[176,128]{1,0:T(8,128)S(1)}, f32[176,128]{1,0:T(8,128)S(1)}, u32[]{:S(2)}, u32[]{:S(2)}) collective-permute-start(f32[176,128]{1,0:T(8,128)S(1)} %add.16), channel_id=1, source_target_pairs={{0,1},{1,2},{2,3},{3,4},{4,5},{5,6},{6,7},{7,0},{8,9},{9,10},{10,1... | collective-permute-start | bytes 270344 | tf_op jit(solution)/shard_map/ppermute | solution.py:339
  66.7 4.3 %collective-permute-start.6 = (f32[176,128]{1,0:T(8,128)S(1)}, f32[176,128]{1,0:T(8,128)S(1)}, u32[]{:S(2)}, u32[]{:S(2)}) collective-permute-start(f32[176,128]{1,0:T(8,128)S(1)} %add.19), channel_id=1, source_target_pairs={{0,7},{1,0},{2,1},{3,2},{4,3},{5,4},{6,5},{7,6},{8,15},{9,8},{10,9... | collective-permute-start | bytes 270344 | tf_op jit(solution)/shard_map/ppermute | solution.py:340
  69.5 4.7 %collective-permute-start.3 = (f32[176,128]{1,0:T(8,128)S(1)}, f32[176,128]{1,0:T(8,128)S(1)}, u32[]{:S(2)}, u32[]{:S(2)}) collective-permute-start(f32[176,128]{1,0:T(8,128)S(1)} %add.17), channel_id=1, source_target_pairs={{0,1},{1,2},{2,3},{3,4},{4,5},{5,6},{6,7},{7,0},{8,9},{9,10},{10,1... | collective-permute-start | bytes 270344 | tf_op jit(solution)/shard_map/ppermute | solution.py:353

commit v3 on v2

v3 whole, which is shorter than its diff:
```python
import functools

import jax
import jax.numpy as jnp
from jax import lax
from jax.experimental import pallas as pl
from jax.experimental.pallas import tpu as pltpu
from jax.sharding import PartitionSpec as P


CAM_ROW = 16
NBR = 14
RANKS = 7
LANES = 128
GROUP = 32
SLOTS = 1024
CHUNKS = SLOTS // LANES
ROWS_IN = 8
ROWS_BACK = 33
SIDE = 144
BLOCK = 176
damping = 1.0
COST = pl.CostEstimate(flops=4_000_000_000, bytes_accessed=4_000_000, transcendentals=0)
PARAMS = pltpu.CompilerParams(vmem_limit_bytes=16 << 20)
F32 = jnp.float32
BF16 = jnp.bfloat16
TILE = (8, LANES)


def lane_groups():
    return lax.broadcasted_iota(jnp.int32, TILE, 1) // GROUP


def regroup(parts, group):
    outs = []
    for a in range(4):
        out = parts[a]
        for b in range(4):
            if b != a:
                out = jnp.where(group == b, pltpu.roll(parts[b], ((b - a) * GROUP) % LANES, 1), out)
        outs.append(out)
    return outs


def ordered(rows, order, d, t):
    idx = jnp.broadcast_to(order[0:1, d * LANES : (d + 1) * LANES], TILE)
    part = idx // LANES
    lane = idx % LANES
    out = None
    for s in range(CHUNKS):
        got = jnp.take_along_axis(rows[t * 8 : t * 8 + 8, s * LANES : (s + 1) * LANES], lane, axis=1)
        out = got if out is None else jnp.where(part == s, got, out)
    return out


def fill_rows(jc, jp, err, cam, rows):
    rows[0:18, :] = jc[...]
    rows[18:24, :] = jp[...]
    rows[24:26, :] = err[...]
    rows[26:27, :] = cam[...].astype(F32)
    rows[27:32, :] = jnp.zeros((5, SLOTS), F32)


def pack_kernel(jc, jp, err, cam, order, msg, rows):
    fill_rows(jc, jp, err, cam, rows)
    group = lane_groups()
    for d in range(CHUNKS):
        tiles = [ordered(rows, order, d, t) for t in range(4)]
        for m, tile in enumerate(regroup(tiles, group)):
            msg[(d * 4 + m) * ROWS_IN : (d * 4 + m) * ROWS_IN + 8, :] = tile


def own_kernel(jc, jp, err, cam, order, own, split, rows):
    fill_rows(jc, jp, err, cam, rows)
    for d in range(CHUNKS):
        cols = slice(d * LANES, (d + 1) * LANES)
        for t in range(4):
            value = ordered(rows, order, d, t)
            own[t * 8 : t * 8 + 8, cols] = value
            if t < 3:
                hi = value.astype(BF16).astype(F32)
                split[t * 8 : t * 8 + 8, cols] = hi
                split[24 + t * 8 : 32 + t * 8, cols] = (value - hi).astype(BF16).astype(F32)


def owner_kernel(owned, partner, msg, slots, turned, near, mixed, back):
    group = lane_groups()
    for r in range(8):
        slots[pl.ds(r, RANKS, stride=8), :] = partner[:, r * LANES : (r + 1) * LANES]
    for row in range(ROWS_IN):
        ins = [owned[pl.ds(m * ROWS_IN + row, 8, stride=4 * ROWS_IN), :] for m in range(4)]
        for t, tile in enumerate(regroup(ins, group)):
            u = t * 8 + row
            if u >= 26:
                continue
            turned[u] = tile
            for b in range(4):
                lanes = pltpu.roll(tile, LANES - b * GROUP, 1) if b else tile
                up = [lanes, pltpu.roll(lanes, 7, 0), pltpu.roll(lanes, 6, 0)] if b else [lanes, pltpu.roll(lanes, 7, 0)]
                for a in range(2):
                    j = a * 4 + b
                    if j:
                        here = jnp.where(group < 4 - b, up[a], up[a + 1]) if b else up[a]
                        turned[j * 52 + u] = here
                        turned[j * 52 + 26 + u] = pltpu.roll(here, 2, 0)
    source = lax.broadcasted_iota(jnp.int32, TILE, 0) * 4 + group
    ranks, words = [], []
    for k in range(RANKS):
        idx = slots[k * 8 : k * 8 + 8, :]
        apart = (idx // GROUP - source) & 31
        ranks.append(apart & 7)
        words.append((idx & 31) + jnp.where(apart < 16, GROUP, 0))

    def picks(j):
        word = jnp.full(TILE, -1, jnp.int32)
        for k in range(RANKS):
            word = jnp.where(ranks[k] == j, words[k], word)
        return word >= 0, group * GROUP + (word & 31), word >= GROUP

    def pick(u, j, lane, ahead):
        front = jnp.take_along_axis(turned[j * 52 + u], lane, axis=1)
        behind = jnp.take_along_axis(turned[j * 52 + 26 + u], lane, axis=1)
        return jnp.where(ahead, front, behind)

    def normal(p, e):
        out = []
        for a in range(3):
            for b in range(a, 3):
                out.append(p[a] * p[b] + p[3 + a] * p[3 + b])
        for a in range(3):
            out.append(p[a] * e[0] + p[3 + a] * e[1])
        return out

    mine = [turned[18 + n] for n in range(8)]
    total = normal(mine[:6], mine[6:])
    for j in range(1, 8):
        valid, lane, ahead = picks(j)
        got = [jnp.where(valid, pick(18 + n, j, lane, ahead), 0.0) for n in range(8)]
        for n in range(6):
            near[(j - 1) * 6 + n] = got[n]
        total = [x + y for x, y in zip(total, normal(got[:6], got[6:]))]
    v00, v01, v02, v11, v12, v22, b0, b1, b2 = total
    i0 = 1.0 / jnp.sqrt(v00 + damping)
    l10 = v01 * i0
    l20 = v02 * i0
    i1 = 1.0 / jnp.sqrt(v11 + damping - l10 * l10)
    l21 = (v12 - l20 * l10) * i1
    i2 = 1.0 / jnp.sqrt(v22 + damping - l20 * l20 - l21 * l21)

    def forward(x0, x1, x2):
        y0 = x0 * i0
        y1 = (x1 - l10 * y0) * i1
        y2 = (x2 - l20 * y0 - l21 * y1) * i2
        return y0, y1, y2

    def inner(x, y):
        return x[0] * y[0] + x[1] * y[1] + x[2] * y[2]

    h = forward(b0, b1, b2)
    g = [forward(*mine[0:3]), forward(*mine[3:6])]
    back[126] = inner(g[0], g[0])
    back[127] = inner(g[0], g[1])
    back[128] = inner(g[1], g[1])
    back[129] = inner(g[0], h)
    back[130] = inner(g[1], h)
    back[131] = jnp.zeros(TILE, F32)

    for j in range(1, 8):
        _, lane, ahead = picks(j)
        p = [near[(j - 1) * 6 + n] for n in range(6)]
        o = [forward(*p[0:3]), forward(*p[3:6])]
        mix = [[-inner(g[a], o[b]) for b in range(2)] for a in range(2)]
        for q in range(9):
            c0 = pick(q, j, lane, ahead)
            c1 = pick(9 + q, j, lane, ahead)
            for a in range(2):
                mixed[(j - 1) * 18 + a * 9 + q] = mix[a][0] * c0 + mix[a][1] * c1
    for k in range(RANKS):
        hits = [ranks[k] == j for j in range(1, 8)]
        for n in range(18):
            out = jnp.zeros(TILE, F32)
            for j in range(7):
                out = jnp.where(hits[j], mixed[j * 18 + n], out)
            back[k * 18 + n] = out
    for row in range(ROWS_BACK):
        tiles = [back[row * 4 + t] for t in range(4)]
        for m, tile in enumerate(regroup(tiles, group)):
            msg[pl.ds(m * ROWS_BACK + row, 8, stride=4 * ROWS_BACK), :] = tile


def build_right(back, own, pair_slot, right_hi, right_lo, flat):
    group = lane_groups()
    low = lax.broadcasted_iota(jnp.int32, TILE, 0)
    for row in range(ROWS_BACK):
        ins = [back[pl.ds(m * ROWS_BACK + row, 8, stride=4 * ROWS_BACK), :] for m in range(4)]
        for t, tile in enumerate(regroup(ins, group)):
            flat[(row * 4 + t) * 8 : (row * 4 + t) * 8 + 8, :] = tile
    for d in range(CHUNKS):
        cols = slice(d * LANES, (d + 1) * LANES)

        def spread(u):
            return jnp.broadcast_to(flat[u * 8 + d : u * 8 + d + 1, :], TILE)

        def mine(u):
            return jnp.broadcast_to(own[u : u + 1, cols], TILE)

        cam = mine(26).astype(jnp.int32)
        m00, m01, m11 = spread(126), spread(127), spread(128)
        grad = [mine(24) - spread(129), mine(25) - spread(130)]
        total = {}
        for q in range(9):
            c0, c1 = mine(q), mine(9 + q)
            diag = [c0 - m00 * c0 - m01 * c1, c1 - m01 * c0 - m11 * c1]
            for i in range(2):
                tail = jnp.where(low == 6, diag[i], 0.0)
                if q == 0:
                    tail = jnp.where(low == 7, grad[i], tail)
                total[q, i, 1] = tail
        for k in range(RANKS):
            slot = jnp.broadcast_to(pair_slot[k : k + 1, cols], TILE)
            o = jnp.where(slot == CAM_ROW * 8 * NBR, -1, slot - cam * NBR)
            hits = [o == low, o == low + 8]
            for q in range(9):
                for i in range(2):
                    n = spread(k * 18 + i * 9 + q)
                    for side in range(2):
                        term = jnp.where(hits[side], n, 0.0)
                        total[q, i, side] = term if (q, i, side) not in total else total[q, i, side] + term
        for q in range(9):
            for i in range(2):
                value = jnp.concatenate([total[q, i, 0], total[q, i, 1]], axis=0)
                hi = value.astype(BF16)
                at = slice((d * 2 + i) * LANES, (d * 2 + i + 1) * LANES)
                right_hi[q * 16 : q * 16 + 16, at] = hi
                right_lo[q * 16 : q * 16 + 16, at] = (value - hi.astype(F32)).astype(BF16)


def dot_t(x, y):
    return lax.dot_general(x, y, (((1,), (1,)), ((), ())), preferred_element_type=F32)


def build_blocks(dests, own, split, right_hi, right_lo, left, wide, outs):
    count = len(dests)
    low = lax.broadcasted_iota(jnp.int32, TILE, 0)
    bases = [(dest * CAM_ROW + low).astype(F32) for dest in dests]
    for d in range(CHUNKS):
        cols = slice(d * LANES, (d + 1) * LANES)
        cam = jnp.broadcast_to(own[26:27, cols], TILE)
        hits = [[cam == base, cam == base + 8.0] for base in bases]
        for i in range(2):
            at = slice((d * 2 + i) * LANES, (d * 2 + i + 1) * LANES)
            for p in range(9):
                for part in range(2):
                    u = part * 24 + i * 9 + p
                    value = jnp.broadcast_to(split[u : u + 1, cols], TILE)
                    for n in range(count):
                        at_row = (part * count + n) * SIDE + p * 16
                        pair = [jnp.where(hit, value, 0.0) for hit in hits[n]]
                        left[at_row : at_row + 16, at] = jnp.concatenate(pair, axis=0).astype(BF16)
    size = count * SIDE
    by_hi = dot_t(left[0 : 2 * size, :], right_hi[...])
    by_lo = dot_t(left[0:size, :], right_lo[...])
    total = by_hi[0:size] + (by_hi[size : 2 * size] + by_lo)
    lane = lax.broadcasted_iota(jnp.int32, (16, LANES), 1)
    for n, out in enumerate(outs):
        block = total[n * SIDE : (n + 1) * SIDE]
        out[0:SIDE, :] = block[:, :LANES]
        wide[:, 0:16] = block[:, LANES:]
        tail = wide[0:16, :]
        for p in range(1, 8):
            tail = jnp.where(lane // 16 == p, pltpu.roll(wide[p * 16 : p * 16 + 16, :], p * 16, 1), tail)
        out[SIDE : SIDE + 16, :] = tail
        out[SIDE + 16 : BLOCK, :] = wide[128:144, :]


def first_kernel(row, back, own, split, pair_slot, block, right_hi, right_lo, left, wide, flat):
    build_right(back, own, pair_slot, right_hi, right_lo, flat)
    wide[...] = jnp.zeros((SIDE, LANES), F32)
    build_blocks([(row[0] + 4) % 8], own, split, right_hi, right_lo, left, wide, [block])


def next_kernel(shifts, row, own, split, right_hi, right_lo, *rest):
    outs, (left, wide) = rest[: len(shifts)], rest[len(shifts) :]
    wide[...] = jnp.zeros((SIDE, LANES), F32)
    build_blocks([(row[0] + s) % 8 for s in shifts], own, split, right_hi, right_lo, left, wide, outs)


def final_kernel(own, plus1, minus1, plus2, minus2, hess, grad, pair, body, last, rows):
    body[...] = own[...] + ((plus1[...] + minus1[...]) + (plus2[...] + minus2[...]))
    for p in range(8):
        piece = body[SIDE : SIDE + 16, :]
        last[p * 16 : p * 16 + 16, :] = piece if p == 0 else pltpu.roll(piece, (LANES - p * 16) % LANES, 1)
    last[128:144, :] = body[SIDE + 16 : BLOCK, :]
    lane = lax.broadcasted_iota(jnp.int32, (9, LANES), 1)
    grads = jnp.zeros((9, LANES), F32)
    for q in range(9):
        halves = [jnp.zeros((9, LANES), F32), jnp.zeros((9, LANES), F32)]
        for c in range(CAM_ROW):
            ref, at = (body, q * 16) if q < 8 else (last, 0)
            x = ref[pl.ds(c, 9, stride=16), :]
            turn = pltpu.roll(x, (c * NBR - at) % LANES, 1)
            for half in range(2):
                lo, hi = c * NBR - half * LANES, (c + 1) * NBR - half * LANES
                if hi > 0 and lo < LANES:
                    halves[half] = jnp.where((lane >= lo) & (lane < hi), turn, halves[half])
            if q == 0:
                grads = jnp.where(lane == c, pltpu.roll(x, (c - at - 15) % LANES, 1), grads)
        for n, x in enumerate(halves):
            rows[pl.ds(n * 88 + q, 9, stride=9), :] = x
    pair[:, 0:LANES] = rows[0:81, :]
    pair[:, LANES : CAM_ROW * NBR] = rows[88:169, : CAM_ROW * NBR - LANES]
    lane = lax.broadcasted_iota(jnp.int32, (16, LANES), 1)
    diag = jnp.zeros((16, LANES), F32)
    for p in range(9):
        for q in range(9):
            ref, at = (body, q * 16) if q < 8 else (last, 0)
            x = ref[p * 16 : p * 16 + 16, :]
            diag = jnp.where(lane == p * 9 + q, pltpu.roll(x, (p * 9 + q - at - 14) % LANES, 1), diag)
    hess[...] = diag[:, :81]
    grad[...] = grads[:, :CAM_ROW]


def on_device(
    camera_jacobian, point_jacobian, residual, send_order, camera_of, track_of, partner, pair_slot
):
    peers = lax.axis_size("obs")
    row = lax.axis_index("row").astype(jnp.int32).reshape(1)
    vmem = pl.BlockSpec(memory_space=pltpu.VMEM)
    smem = pl.BlockSpec(memory_space=pltpu.SMEM)
    raw = (camera_jacobian, point_jacobian, residual, camera_of.reshape(1, SLOTS), send_order.reshape(1, SLOTS))
    msg = pl.pallas_call(
        pack_kernel,
        out_shape=jax.ShapeDtypeStruct((peers * ROWS_IN, LANES), F32),
        scratch_shapes=[pltpu.VMEM((32, SLOTS), F32)],
        name="pack",
    )(*raw)
    owned = lax.all_to_all(msg.reshape(peers, ROWS_IN, LANES), "obs", 0, 0, tiled=True)
    returned = pl.pallas_call(
        owner_kernel,
        out_shape=jax.ShapeDtypeStruct((peers * ROWS_BACK, LANES), F32),
        scratch_shapes=[
            pltpu.VMEM((RANKS * 8, LANES), jnp.int32),
            pltpu.VMEM((8 * 52, 8, LANES), F32),
            pltpu.VMEM((RANKS * 6, 8, LANES), F32),
            pltpu.VMEM((RANKS * 18, 8, LANES), F32),
            pltpu.VMEM((132, 8, LANES), F32),
        ],
        compiler_params=PARAMS,
        name="owner",
    )(owned.reshape(peers * ROWS_IN, LANES), partner)
    back = lax.all_to_all(returned.reshape(peers, 1, ROWS_BACK * LANES), "obs", 0, 0, tiled=True)
    block = jax.ShapeDtypeStruct((BLOCK, LANES), F32)
    side = jax.ShapeDtypeStruct((SIDE, 2 * SLOTS), BF16)
    own, split = pl.pallas_call(
        own_kernel,
        out_shape=(jax.ShapeDtypeStruct((32, SLOTS), F32), jax.ShapeDtypeStruct((48, SLOTS), F32)),
        scratch_shapes=[pltpu.VMEM((32, SLOTS), F32)],
        compiler_params=PARAMS,
        cost_estimate=COST,
        name="own",
    )(*raw)

    def scratch(count):
        return [pltpu.VMEM((2 * count * SIDE, 2 * SLOTS), BF16), pltpu.VMEM((SIDE, LANES), F32)]

    far, right_hi, right_lo = pl.pallas_call(
        first_kernel,
        in_specs=[smem, vmem, vmem, vmem, vmem],
        out_shape=(block, side, side),
        scratch_shapes=scratch(1) + [pltpu.VMEM((132 * 8, LANES), F32)],
        compiler_params=PARAMS,
        cost_estimate=COST,
        name="camera_0",
    )(row, back.reshape(peers * ROWS_BACK, LANES), own, split, pair_slot)

    def blocks(shifts):
        return pl.pallas_call(
            functools.partial(next_kernel, shifts),
            in_specs=[smem, vmem, vmem, vmem, vmem],
            out_shape=(block,) * len(shifts),
            scratch_shapes=scratch(len(shifts)),
            compiler_params=PARAMS,
            cost_estimate=COST,
        )(row, own, split, right_hi, right_lo)

    def shift(x, by):
        return lax.ppermute(x, "row", [(n, (n + by) % 8) for n in range(8)])

    far = shift(far, 2)
    plus, minus = blocks((3, 5))
    plus, minus = shift(plus, 1), shift(minus, -1)
    plus2, minus2 = blocks((2, 6))
    plus1, minus1 = blocks((1, 7))
    plus2 = shift(plus2 + (plus + far), 2)
    minus2 = shift(minus2 + minus, -2)
    plus1, minus1 = shift(plus1, 1), shift(minus1, -1)
    (kept,) = blocks((0,))
    hess, grad, pair = pl.pallas_call(
        final_kernel,
        out_shape=(
            jax.ShapeDtypeStruct((CAM_ROW, 81), F32),
            jax.ShapeDtypeStruct((9, CAM_ROW), F32),
            jax.ShapeDtypeStruct((81, CAM_ROW * NBR), F32),
        ),
        scratch_shapes=[
            pltpu.VMEM((BLOCK, LANES), F32),
            pltpu.VMEM((SIDE, LANES), F32),
            pltpu.VMEM((176, LANES), F32),
        ],
        compiler_params=PARAMS,
        name="final",
    )(kept, plus1, minus1, plus2, minus2)
    return hess.T, grad, pair


def solution(mesh):
    return jax.shard_map(
        on_device,
        mesh=mesh,
        in_specs=(
            P(None, ("obs", "row")),
            P(None, ("obs", "row")),
            P(None, ("obs", "row")),
            P(("obs", "row")),
            P(("obs", "row")),
            P(("obs", "row")),
            P(None, ("obs", "row")),
            P(None, ("obs", "row")),
        ),
        out_specs=(P(None, ("obs", "row")), P(None, ("obs", "row")), P(None, ("obs", "row"))),
        check_vma=False,
    )
```

time: 75.7 us -> 65.1 us (0.86)
  the two profiles are of different devices: /device:TPU:1 before, /device:TPU:32 now
where the time goes in v3:
time: 65.1 us; the launch traced here: 64.7 us
  waiting for transfers between devices  20.1 us (31%)
  blocking collectives  15.3 us (24%)
  starting transfers between devices  15 us (23%)
  Pallas kernels  12.9 us (20%)
  between operations  0.72 us (1%)
  local copies, waits for them, and re-layouts  0.66 us (1%)
    all_to_all x1, blocking collectives, on_device(): lax.all_to_all(msg.reshape(peers, ROWS_IN, LANES), 'obs', 0, 0, tiled=True)  15.3 us
    ppermute x7, starting transfers between devices, shift(): return lax.ppermute(x, 'row', [(n, (n + by) % 8) for n in range(8)])  11 us
    all_to_all x1, waiting for transfers between devices, on_device(): lax.all_to_all(returned.reshape(peers, 1, ROWS_BACK * LANES), 'obs', 0, 0...  10.1 us
    ppermute x7, waiting for transfers between devices, shift(): return lax.ppermute(x, 'row', [(n, (n + by) % 8) for n in range(8)])  9.98 us
    pallas_call x4, Pallas kernels, blocks(): pl.pallas_call(functools.partial(next_kernel, shifts), in_specs=[smem, vm...  4.35 us
    all_to_all x1, starting transfers between devices, on_device(): lax.all_to_all(returned.reshape(peers, 1, ROWS_BACK * LANES), 'obs', 0, 0...  4.03 us
    pallas_call x1, Pallas kernels, on_device(): pl.pallas_call(pack_kernel, out_shape=jax.ShapeDtypeStruct((peers * ROWS_...  2.47 us
    pallas_call x1, Pallas kernels, on_device(): pl.pallas_call(owner_kernel, out_shape=jax.ShapeDtypeStruct((peers * ROWS...  2.42 us
  transfers between devices with their start and end apart: 8, of which 4 were waited for; matrix products, arithmetic and copies ran while one was open for 0% of the time, Pallas kernels for 4%

profile of v3, /device:TPU:32, one launch (start us, length us, event | category | flops | bytes accessed | tf_op | source)
XLA Modules:
  0.0 64.7 jit_solution(4298819953741229351)
XLA Ops:
  0.6 2.5 %pack.1 = f32[256,128]{1,0:T(8,128)} custom-call(f32[18,1024]{1,0:T(8,128)} %jc.3, f32[6,1024]{1,0:T(8,128)} %jp.3, f32[2,1024]{1,0:T(2,128)} %err.3, s32[1,1024]{1,0:T(1,128)} %bitcast.10, s32[1,1024]{1,0:T(1,128)} %bitcast.12), custom_call_target="tpu_custom_call" | custom-call | tf_op jit(solution)/shard_map/pack/pallas_call | solution.py:331
  3.1 0.0 copy-start.1
  3.1 15.3 %all_to_all.10 = f32[32,8,128]{2,1,0:T(8,128)S(1)} all-to-all(f32[32,8,128]{2,1,0:T(8,128)} %bitcast.14), channel_id=1, replica_groups=mesh['obs'=32,'row'=8] {'obs'}, dimensions={0} | all-to-all | bytes 262144 | tf_op jit(solution)/shard_map/all_to_all | solution.py:337
  18.4 0.0 copy-done.1
  18.4 2.4 %owner.1 = f32[1056,128]{1,0:T(8,128)} custom-call(f32[256,128]{1,0:T(8,128)S(1)} %bitcast.9, s32[7,1024]{1,0:T(8,128)S(1)} %copy-done.1), custom_call_target="tpu_custom_call" | custom-call | tf_op jit(solution)/shard_map/owner/pallas_call | solution.py:338
  20.8 0.0 copy-start
  20.8 0.0 copy-start.2
  20.8 0.0 copy-start.3
  20.8 0.0 copy-start.5
  20.8 4.0 %all-to-all-start.1 = ((f32[32,1,4224]{2,1,0:T(1,128)}), f32[32,1,4224]{2,1,0:T(1,128)S(1)}, u32[]{:S(2)}, u32[]{:S(2)}) async-start(f32[32,1,4224]{2,1,0:T(1,128)} %bitcast.5), calls=%async_computation.1 | async-start | bytes 1081344 | tf_op jit(solution)/shard_map/all_to_all | solution.py:351
  24.9 0.0 copy-start.4
  24.9 0.0 copy-done
  24.9 0.0 copy-done.2
  24.9 0.0 copy-done.3
  24.9 0.0 copy-done.5
  24.9 0.6 copy-done.4
  25.6 0.0 copy-start.6
  25.6 0.5 own.1
  26.0 10.1 %all-to-all-done.1 = f32[32,1,4224]{2,1,0:T(1,128)S(1)} async-done(((f32[32,1,4224]{2,1,0:T(1,128)}), f32[32,1,4224]{2,1,0:T(1,128)S(1)}, u32[]{:S(2)}, u32[]{:S(2)}) %all-to-all-start.1) | async-done | bytes 540704 | tf_op jit(solution)/shard_map/all_to_all | solution.py:351
  36.1 0.0 copy-done.6
  36.1 2.0 %camera_0.1 = (f32[176,128]{1,0:T(8,128)S(1)}, bf16[144,2048]{1,0:T(8,128)(2,1)S(1)}, bf16[144,2048]{1,0:T(8,128)(2,1)S(1)}) custom-call(s32[1]{0:T(128)} %bitcast.row, f32[1056,128]{1,0:T(8,128)S(1)} %bitcast.8, f32[32,1024]{1,0:T(8,128)S(1)} %get-tuple-element.17.own, f32[48,1024]{1,0:T(8,128)S(1)} %get-tuple-element.18.split, s32[7,1024]{1,0:T(8,128)S(1)} %copy-done.6), custom_call_target="tpu_custom_call" | custom-call | flops 4000000000 | bytes 4000000 | tf_op jit(solution)/shard_map/camera_0/pallas_call | solution.py:366
  38.1 1.2 %shard_map.97 = (f32[176,128]{1,0:T(8,128)S(1)}, f32[176,128]{1,0:T(8,128)S(1)}) custom-call(s32[1]{0:T(128)} %bitcast.row, f32[32,1024]{1,0:T(8,128)S(1)} %get-tuple-element.17.own, f32[48,1024]{1,0:T(8,128)S(1)} %get-tuple-element.18.split, bf16[144,2048]{1,0:T(8,128)(2,1)S(1)} %get-tuple-element.19.right_hi, bf16[144,2048]{1,0:T(8,128)(2,1)S(1)} %get-tuple-element.20.right_lo), custom_call_target="tpu_custom_call" | custom-call | flops 4000000000 | bytes 4000000 | tf_op jit(solution)/shard_map/pallas_call | solution.py:377
  39.3 1.2 %shard_map.96 = (f32[176,128]{1,0:T(8,128)S(1)}, f32[176,128]{1,0:T(8,128)S(1)}) custom-call(s32[1]{0:T(128)} %bitcast.row, f32[32,1024]{1,0:T(8,128)S(1)} %get-tuple-element.17.own, f32[48,1024]{1,0:T(8,128)S(1)} %get-tuple-element.18.split, bf16[144,2048]{1,0:T(8,128)(2,1)S(1)} %get-tuple-element.19.right_hi, bf16[144,2048]{1,0:T(8,128)(2,1)S(1)} %get-tuple-element.20.right_lo), custom_call_target="tpu_custom_call" | custom-call | flops 4000000000 | bytes 4000000 | tf_op jit(solution)/shard_map/pallas_call | solution.py:377
  40.5 0.2 collective-permute-start.5
  40.7 1.9 %collective-permute-start.2 = (f32[176,128]{1,0:T(8,128)S(1)}, f32[176,128]{1,0:T(8,128)S(1)}, u32[]{:S(2)}, u32[]{:S(2)}) collective-permute-start(f32[176,128]{1,0:T(8,128)S(1)} %get-tuple-element.24), channel_id=1, source_target_pairs={{0,1},{1,2},{2,3},{3,4},{4,5},{5,6},{6,7},{7,0},{8,9},{9,10},{10,1... | collective-permute-start | bytes 270344 | tf_op jit(solution)/shard_map/ppermute | solution.py:387
  42.6 4.5 %collective-permute-start.3 = (f32[176,128]{1,0:T(8,128)S(1)}, f32[176,128]{1,0:T(8,128)S(1)}, u32[]{:S(2)}, u32[]{:S(2)}) collective-permute-start(f32[176,128]{1,0:T(8,128)S(1)} %get-tuple-element.25), channel_id=1, source_target_pairs={{0,2},{1,3},{2,4},{3,5},{4,6},{5,7},{6,0},{7,1},{8,10},{9,11},{10,... | collective-permute-start | bytes 270344 | tf_op jit(solution)/shard_map/ppermute | solution.py:387
  47.1 1.2 %shard_map.95 = (f32[176,128]{1,0:T(8,128)S(1)}, f32[176,128]{1,0:T(8,128)S(1)}) custom-call(s32[1]{0:T(128)} %bitcast.row, f32[32,1024]{1,0:T(8,128)S(1)} %get-tuple-element.17.own, f32[48,1024]{1,0:T(8,128)S(1)} %get-tuple-element.18.split, bf16[144,2048]{1,0:T(8,128)(2,1)S(1)} %get-tuple-element.19.right_hi, bf16[144,2048]{1,0:T(8,128)(2,1)S(1)} %get-tuple-element.20.right_lo), custom_call_target="tpu_custom_call" | custom-call | flops 4000000000 | bytes 4000000 | tf_op jit(solution)/shard_map/pallas_call | solution.py:377
  48.3 2.0 %collective-permute-start = (f32[176,128]{1,0:T(8,128)S(1)}, f32[176,128]{1,0:T(8,128)S(1)}, u32[]{:S(2)}, u32[]{:S(2)}) collective-permute-start(f32[176,128]{1,0:T(8,128)S(1)} %get-tuple-element.21), channel_id=1, source_target_pairs={{0,1},{1,2},{2,3},{3,4},{4,5},{5,6},{6,7},{7,0},{8,9},{9,10},{10,1... | collective-permute-start | bytes 270344 | tf_op jit(solution)/shard_map/ppermute | solution.py:387
  50.3 0.1 collective-permute-start.1
  50.4 0.0 collective-permute-done.5
  50.4 2.2 %collective-permute-start.6 = (f32[176,128]{1,0:T(8,128)S(1)}, f32[176,128]{1,0:T(8,128)S(1)}, u32[]{:S(2)}, u32[]{:S(2)}) collective-permute-start(f32[176,128]{1,0:T(8,128)S(1)} %add.11), channel_id=1, source_target_pairs={{0,6},{1,7},{2,0},{3,1},{4,2},{5,3},{6,4},{7,5},{8,14},{9,15},{10,... | collective-permute-start | bytes 270344 | tf_op jit(solution)/shard_map/ppermute | solution.py:387
  52.6 0.0 collective-permute-done.2
  52.6 3.9 %collective-permute-done.3 = f32[176,128]{1,0:T(8,128)S(1)} collective-permute-done((f32[176,128]{1,0:T(8,128)S(1)}, f32[176,128]{1,0:T(8,128)S(1)}, u32[]{:S(2)}, u32[]{:S(2)}) %collective-permute-start.3) | collective-permute-done | bytes 90144 | tf_op jit(solution)/shard_map/ppermute | solution.py:387
  56.6 0.1 collective-permute-start.4
  56.7 0.8 %shard_map.94.own = f32[176,128]{1,0:T(8,128)S(1)} custom-call(s32[1]{0:T(128)} %bitcast.row, f32[32,1024]{1,0:T(8,128)S(1)} %get-tuple-element.17.own, f32[48,1024]{1,0:T(8,128)S(1)} %get-tuple-element.18.split, bf16[144,2048]{1,0:T(8,128)(2,1)S(1)} %get-tuple-element.19.right_hi, bf16[144,2048]{1,0:T(8,128)(2,1)S(1)} %get-tuple-element.20.right_lo), custom_call_target="tpu_custom_call" | custom-call | flops 4000000000 | bytes 4000000 | tf_op jit(solution)/shard_map/pallas_call | solution.py:377
  57.4 0.0 collective-permute-done.plus1
  57.4 0.0 collective-permute-done.1.minus1
  57.4 0.1 collective-permute-done.6.minus2
  57.5 6.0 %collective-permute-done.4.plus2 = f32[176,128]{1,0:T(8,128)S(1)} collective-permute-done((f32[176,128]{1,0:T(8,128)S(1)}, f32[176,128]{1,0:T(8,128)S(1)}, u32[]{:S(2)}, u32[]{:S(2)}) %collective-permute-start.4) | collective-permute-done | bytes 90144 | tf_op jit(solution)/shard_map/ppermute | solution.py:387
  63.5 1.2 %final.1 = (f32[16,81]{1,0:T(8,128)}, f32[9,16]{1,0:T(8,128)}, f32[81,224]{1,0:T(8,128)}) custom-call(f32[176,128]{1,0:T(8,128)S(1)} %shard_map.94.own, f32[176,128]{1,0:T(8,128)S(1)} %collective-permute-done.plus1, f32[176,128]{1,0:T(8,128)S(1)} %collective-permute-done.1.minus1, f32[176,128]{1,0:T(8,128)S(1)} %collective-permute-done.4.plus2, ...), custom_call_target="tpu_custom_call" | custom-call | tf_op jit(solution)/shard_map/final/pallas_call | solution.py:398
  (2 shorter events, 0.0 us)
Async XLA Ops:
  3.1 15.3 %copy-start.1 = (s32[7,1024]{1,0:T(8,128)S(1)}, s32[7,1024]{1,0:T(8,128)}, u32[]{:S(2)}) copy-start(s32[7,1024]{1,0:T(8,128)} %partner.1) | copy-start | bytes 86020
  20.8 4.1 %copy-start = (f32[18,1024]{1,0:T(8,128)S(1)}, f32[18,1024]{1,0:T(8,128)}, u32[]{:S(2)}) copy-start(f32[18,1024]{1,0:T(8,128)} %jc.3) | copy-start | bytes 221188
  20.8 4.1 %copy-start.2 = (f32[6,1024]{1,0:T(8,128)S(1)}, f32[6,1024]{1,0:T(8,128)}, u32[]{:S(2)}) copy-start(f32[6,1024]{1,0:T(8,128)} %jp.3) | copy-start | bytes 73732
  20.8 4.1 %copy-start.3 = (f32[2,1024]{1,0:T(2,128)S(1)}, f32[2,1024]{1,0:T(2,128)}, u32[]{:S(2)}) copy-start(f32[2,1024]{1,0:T(2,128)} %err.3) | copy-start | bytes 24580
  20.8 4.1 %copy-start.5 = (s32[1024]{0:T(1024)S(1)}, s32[1024]{0:T(1024)}, u32[]{:S(2)}) copy-start(s32[1024]{0:T(1024)} %param.11) | copy-start | bytes 12292
  20.8 15.3 %all-to-all-start.1 = ((f32[32,1,4224]{2,1,0:T(1,128)}), f32[32,1,4224]{2,1,0:T(1,128)S(1)}, u32[]{:S(2)}, u32[]{:S(2)}) async-start(f32[32,1,4224]{2,1,0:T(1,128)} %bitcast.5), calls=%async_computation.1 | async-start | bytes 1081344 | tf_op jit(solution)/shard_map/all_to_all | solution.py:351
  24.9 0.7 %copy-start.4 = (s32[1024]{0:T(1024)S(1)}, s32[1024]{0:T(1024)}, u32[]{:S(2)}) copy-start(s32[1024]{0:T(1024)} %param.12) | copy-start | bytes 12292
  25.6 10.5 %copy-start.6 = (s32[7,1024]{1,0:T(8,128)S(1)}, s32[7,1024]{1,0:T(8,128)}, u32[]{:S(2)}) copy-start(s32[7,1024]{1,0:T(8,128)} %pair_slot.1) | copy-start | bytes 86020
  40.5 9.9 %collective-permute-start.5 = (f32[176,128]{1,0:T(8,128)S(1)}, f32[176,128]{1,0:T(8,128)S(1)}, u32[]{:S(2)}, u32[]{:S(2)}) collective-permute-start(f32[176,128]{1,0:T(8,128)S(1)} %get-tuple-element.27), channel_id=1, source_target_pairs={{0,7},{1,0},{2,1},{3,2},{4,3},{5,4},{6,5},{7,6},{8,15},{9,8},{10,9... | collective-permute-start | bytes 270344 | tf_op jit(solution)/shard_map/ppermute | solution.py:387
  40.7 11.9 %collective-permute-start.2 = (f32[176,128]{1,0:T(8,128)S(1)}, f32[176,128]{1,0:T(8,128)S(1)}, u32[]{:S(2)}, u32[]{:S(2)}) collective-permute-start(f32[176,128]{1,0:T(8,128)S(1)} %get-tuple-element.24), channel_id=1, source_target_pairs={{0,1},{1,2},{2,3},{3,4},{4,5},{5,6},{6,7},{7,0},{8,9},{9,10},{10,1... | collective-permute-start | bytes 270344 | tf_op jit(solution)/shard_map/ppermute | solution.py:387
  42.6 13.9 %collective-permute-start.3 = (f32[176,128]{1,0:T(8,128)S(1)}, f32[176,128]{1,0:T(8,128)S(1)}, u32[]{:S(2)}, u32[]{:S(2)}) collective-permute-start(f32[176,128]{1,0:T(8,128)S(1)} %get-tuple-element.25), channel_id=1, source_target_pairs={{0,2},{1,3},{2,4},{3,5},{4,6},{5,7},{6,0},{7,1},{8,10},{9,11},{10,... | collective-permute-start | bytes 270344 | tf_op jit(solution)/shard_map/ppermute | solution.py:387
  48.3 9.1 %collective-permute-start = (f32[176,128]{1,0:T(8,128)S(1)}, f32[176,128]{1,0:T(8,128)S(1)}, u32[]{:S(2)}, u32[]{:S(2)}) collective-permute-start(f32[176,128]{1,0:T(8,128)S(1)} %get-tuple-element.21), channel_id=1, source_target_pairs={{0,1},{1,2},{2,3},{3,4},{4,5},{5,6},{6,7},{7,0},{8,9},{9,10},{10,1... | collective-permute-start | bytes 270344 | tf_op jit(solution)/shard_map/ppermute | solution.py:387
  50.3 7.1 %collective-permute-start.1 = (f32[176,128]{1,0:T(8,128)S(1)}, f32[176,128]{1,0:T(8,128)S(1)}, u32[]{:S(2)}, u32[]{:S(2)}) collective-permute-start(f32[176,128]{1,0:T(8,128)S(1)} %get-tuple-element.22), channel_id=1, source_target_pairs={{0,7},{1,0},{2,1},{3,2},{4,3},{5,4},{6,5},{7,6},{8,15},{9,8},{10,9... | collective-permute-start | bytes 270344 | tf_op jit(solution)/shard_map/ppermute | solution.py:387
  50.4 7.1 %collective-permute-start.6 = (f32[176,128]{1,0:T(8,128)S(1)}, f32[176,128]{1,0:T(8,128)S(1)}, u32[]{:S(2)}, u32[]{:S(2)}) collective-permute-start(f32[176,128]{1,0:T(8,128)S(1)} %add.11), channel_id=1, source_target_pairs={{0,6},{1,7},{2,0},{3,1},{4,2},{5,3},{6,4},{7,5},{8,14},{9,15},{10,... | collective-permute-start | bytes 270344 | tf_op jit(solution)/shard_map/ppermute | solution.py:387
  56.6 6.9 %collective-permute-start.4 = (f32[176,128]{1,0:T(8,128)S(1)}, f32[176,128]{1,0:T(8,128)S(1)}, u32[]{:S(2)}, u32[]{:S(2)}) collective-permute-start(f32[176,128]{1,0:T(8,128)S(1)} %add_add_fusion), channel_id=1, source_target_pairs={{0,2},{1,3},{2,4},{3,5},{4,6},{5,7},{6,0},{7,1},{8,10},{9,11},{10,... | collective-permute-start | bytes 270344 | tf_op jit(solution)/shard_map/ppermute | solution.py:387

commit v4 on v3

--- a/solution.py
+++ b/solution.py
@@ -61,7 +61,14 @@
     rows[27:32, :] = jnp.zeros((5, SLOTS), F32)
 
 
-def pack_kernel(jc, jp, err, cam, order, msg, rows):
+def pack_kernel(*refs):
+    sources, (msg, rows, *targets, sems) = refs[:5], refs[5:]
+    copies = [pltpu.make_async_copy(x, y, sems.at[n]) for n, (x, y) in enumerate(zip(sources, targets))]
+    for copy in copies:
+        copy.start()
+    for copy in copies:
+        copy.wait()
+    jc, jp, err, cam, order = targets
     fill_rows(jc, jp, err, cam, rows)
     group = lane_groups()
     for d in range(CHUNKS):
@@ -184,17 +191,22 @@
             back[k * 18 + n] = out
     for row in range(ROWS_BACK):
         tiles = [back[row * 4 + t] for t in range(4)]
-        for m, tile in enumerate(regroup(tiles, group)):
-            msg[pl.ds(m * ROWS_BACK + row, 8, stride=4 * ROWS_BACK), :] = tile
-
-
-def build_right(back, own, pair_slot, right_hi, right_lo, flat):
+        tiles = [pltpu.roll(tile, t * GROUP, 1) if t else tile for t, tile in enumerate(tiles)]
+        for m in range(4):
+            out = tiles[0]
+            for t in range(1, 4):
+                out = jnp.where(group == (t + m) % 4, tiles[t], out)
+            msg[pl.ds(m * ROWS_BACK + row, 8, stride=4 * ROWS_BACK), :] = out
+
+
+def build_right(turn, back, own, pair_slot, right_hi, right_lo, flat):
     group = lane_groups()
     low = lax.broadcasted_iota(jnp.int32, TILE, 0)
     for row in range(ROWS_BACK):
         ins = [back[pl.ds(m * ROWS_BACK + row, 8, stride=4 * ROWS_BACK), :] for m in range(4)]
         for t, tile in enumerate(regroup(ins, group)):
-            flat[(row * 4 + t) * 8 : (row * 4 + t) * 8 + 8, :] = tile
+            at = row * 32 + ((t - turn) & 3) * 8
+            flat[pl.ds(pl.multiple_of(at, 8), 8), :] = tile
     for d in range(CHUNKS):
         cols = slice(d * LANES, (d + 1) * LANES)
 
@@ -226,13 +238,14 @@
                     for side in range(2):
                         term = jnp.where(hits[side], n, 0.0)
                         total[q, i, side] = term if (q, i, side) not in total else total[q, i, side] + term
+        wide = slice(d * 2 * LANES, (d + 1) * 2 * LANES)
         for q in range(9):
-            for i in range(2):
-                value = jnp.concatenate([total[q, i, 0], total[q, i, 1]], axis=0)
+            for side in range(2):
+                value = jnp.concatenate([total[q, 0, side], total[q, 1, side]], axis=1)
                 hi = value.astype(BF16)
-                at = slice((d * 2 + i) * LANES, (d * 2 + i + 1) * LANES)
-                right_hi[q * 16 : q * 16 + 16, at] = hi
-                right_lo[q * 16 : q * 16 + 16, at] = (value - hi.astype(F32)).astype(BF16)
+                at = slice(q * 16 + side * 8, q * 16 + side * 8 + 8)
+                right_hi[at, wide] = hi
+                right_lo[at, wide] = (value - hi.astype(F32)).astype(BF16)
 
 
 def dot_t(x, y):
@@ -247,16 +260,15 @@
         cols = slice(d * LANES, (d + 1) * LANES)
         cam = jnp.broadcast_to(own[26:27, cols], TILE)
         hits = [[cam == base, cam == base + 8.0] for base in bases]
-        for i in range(2):
-            at = slice((d * 2 + i) * LANES, (d * 2 + i + 1) * LANES)
-            for p in range(9):
-                for part in range(2):
-                    u = part * 24 + i * 9 + p
-                    value = jnp.broadcast_to(split[u : u + 1, cols], TILE)
-                    for n in range(count):
-                        at_row = (part * count + n) * SIDE + p * 16
-                        pair = [jnp.where(hit, value, 0.0) for hit in hits[n]]
-                        left[at_row : at_row + 16, at] = jnp.concatenate(pair, axis=0).astype(BF16)
+        span = slice(d * 2 * LANES, (d + 1) * 2 * LANES)
+        for p in range(9):
+            for part in range(2):
+                values = [jnp.broadcast_to(split[u : u + 1, cols], TILE) for u in (part * 24 + p, part * 24 + 9 + p)]
+                for n in range(count):
+                    for side in range(2):
+                        at = (part * count + n) * SIDE + p * 16 + side * 8
+                        both = [jnp.where(hits[n][side], value, 0.0) for value in values]
+                        left[at : at + 8, span] = jnp.concatenate(both, axis=1).astype(BF16)
     size = count * SIDE
     by_hi = dot_t(left[0 : 2 * size, :], right_hi[...])
     by_lo = dot_t(left[0:size, :], right_lo[...])
@@ -273,16 +285,16 @@
         out[SIDE + 16 : BLOCK, :] = wide[128:144, :]
 
 
-def first_kernel(row, back, own, split, pair_slot, block, right_hi, right_lo, left, wide, flat):
-    build_right(back, own, pair_slot, right_hi, right_lo, flat)
+def first_kernel(back, own, split, pair_slot, block, right_hi, right_lo, left, wide, flat):
+    build_right(lax.axis_index("obs") & 3, back, own, pair_slot, right_hi, right_lo, flat)
     wide[...] = jnp.zeros((SIDE, LANES), F32)
-    build_blocks([(row[0] + 4) % 8], own, split, right_hi, right_lo, left, wide, [block])
-
-
-def next_kernel(shifts, row, own, split, right_hi, right_lo, *rest):
+    build_blocks([(lax.axis_index("row") + 4) & 7], own, split, right_hi, right_lo, left, wide, [block])
+
+
+def next_kernel(shifts, own, split, right_hi, right_lo, *rest):
     outs, (left, wide) = rest[: len(shifts)], rest[len(shifts) :]
     wide[...] = jnp.zeros((SIDE, LANES), F32)
-    build_blocks([(row[0] + s) % 8 for s in shifts], own, split, right_hi, right_lo, left, wide, outs)
+    build_blocks([(lax.axis_index("row") + s) & 7 for s in shifts], own, split, right_hi, right_lo, left, wide, outs)
 
 
 def final_kernel(own, plus1, minus1, plus2, minus2, hess, grad, pair, body, last, rows):
@@ -309,14 +321,17 @@
             rows[pl.ds(n * 88 + q, 9, stride=9), :] = x
     pair[:, 0:LANES] = rows[0:81, :]
     pair[:, LANES : CAM_ROW * NBR] = rows[88:169, : CAM_ROW * NBR - LANES]
-    lane = lax.broadcasted_iota(jnp.int32, (16, LANES), 1)
-    diag = jnp.zeros((16, LANES), F32)
-    for p in range(9):
-        for q in range(9):
-            ref, at = (body, q * 16) if q < 8 else (last, 0)
-            x = ref[p * 16 : p * 16 + 16, :]
-            diag = jnp.where(lane == p * 9 + q, pltpu.roll(x, (p * 9 + q - at - 14) % LANES, 1), diag)
-    hess[...] = diag[:, :81]
+    lane = lax.broadcasted_iota(jnp.int32, TILE, 1)
+    for half in range(2):
+        diag = jnp.zeros(TILE, F32)
+        for p in range(9):
+            at = p * 16 + half * 8
+            q = lane - p * 9
+            x = jnp.take_along_axis(body[at : at + 8, :], (q * 16 + 14) & (LANES - 1), axis=1)
+            diag = jnp.where((q >= 0) & (q < 8), x, diag)
+            x = pltpu.roll(last[at : at + 8, :], (p * 9 + 8 - 14) % LANES, 1)
+            diag = jnp.where(q == 8, x, diag)
+        hess[half * 8 : half * 8 + 8, :] = diag[:, :81]
     grad[...] = grads[:, :CAM_ROW]
 
 
@@ -324,16 +339,24 @@
     camera_jacobian, point_jacobian, residual, send_order, camera_of, track_of, partner, pair_slot
 ):
     peers = lax.axis_size("obs")
-    row = lax.axis_index("row").astype(jnp.int32).reshape(1)
-    vmem = pl.BlockSpec(memory_space=pltpu.VMEM)
-    smem = pl.BlockSpec(memory_space=pltpu.SMEM)
-    raw = (camera_jacobian, point_jacobian, residual, camera_of.reshape(1, SLOTS), send_order.reshape(1, SLOTS))
+    order = send_order.reshape(1, SLOTS)
+    raw = (camera_jacobian, point_jacobian, residual, camera_of.reshape(1, SLOTS), order)
     msg = pl.pallas_call(
         pack_kernel,
         out_shape=jax.ShapeDtypeStruct((peers * ROWS_IN, LANES), F32),
-        scratch_shapes=[pltpu.VMEM((32, SLOTS), F32)],
+        in_specs=[pl.BlockSpec(memory_space=pltpu.HBM)] * 5,
+        scratch_shapes=[
+            pltpu.VMEM((32, SLOTS), F32),
+            pltpu.VMEM((18, SLOTS), F32),
+            pltpu.VMEM((6, SLOTS), F32),
+            pltpu.VMEM((2, SLOTS), F32),
+            pltpu.VMEM((1, SLOTS), jnp.int32),
+            pltpu.VMEM((1, SLOTS), jnp.int32),
+            pltpu.SemaphoreType.DMA((5,)),
+        ],
+        compiler_params=PARAMS,
         name="pack",
-    )(*raw)
+    )(*[pltpu.with_memory_space_constraint(x, pltpu.HBM) for x in raw])
     owned = lax.all_to_all(msg.reshape(peers, ROWS_IN, LANES), "obs", 0, 0, tiled=True)
     returned = pl.pallas_call(
         owner_kernel,
@@ -365,23 +388,21 @@
 
     far, right_hi, right_lo = pl.pallas_call(
         first_kernel,
-        in_specs=[smem, vmem, vmem, vmem, vmem],
         out_shape=(block, side, side),
         scratch_shapes=scratch(1) + [pltpu.VMEM((132 * 8, LANES), F32)],
         compiler_params=PARAMS,
         cost_estimate=COST,
         name="camera_0",
-    )(row, back.reshape(peers * ROWS_BACK, LANES), own, split, pair_slot)
+    )(back.reshape(peers * ROWS_BACK, LANES), own, split, pair_slot)
 
     def blocks(shifts):
         return pl.pallas_call(
             functools.partial(next_kernel, shifts),
-            in_specs=[smem, vmem, vmem, vmem, vmem],
-            out_shape=(block,) * len(shifts),
+                out_shape=(block,) * len(shifts),
             scratch_shapes=scratch(len(shifts)),
             compiler_params=PARAMS,
             cost_estimate=COST,
-        )(row, own, split, right_hi, right_lo)
+        )(own, split, right_hi, right_lo)
 
     def shift(x, by):
         return lax.ppermute(x, "row", [(n, (n + by) % 8) for n in range(8)])

time: 65.1 us -> 63.5 us (0.975)
  Pallas kernels: 12.9 us -> 11.6 us
where the time goes in v4:
time: 63.5 us; the launch traced here: 63.2 us
  waiting for transfers between devices  20.7 us (33%)
  blocking collectives  15 us (24%)
  starting transfers between devices  15 us (24%)
  Pallas kernels  11.6 us (18%)
  between operations  0.75 us (1%)
    all_to_all x1, blocking collectives, on_device(): lax.all_to_all(msg.reshape(peers, ROWS_IN, LANES), 'obs', 0, 0, tiled=True)  15 us
    ppermute x7, starting transfers between devices, shift(): return lax.ppermute(x, 'row', [(n, (n + by) % 8) for n in range(8)])  11 us
    all_to_all x1, waiting for transfers between devices, on_device(): lax.all_to_all(returned.reshape(peers, 1, ROWS_BACK * LANES), 'obs', 0, 0...  10.7 us
    ppermute x7, waiting for transfers between devices, shift(): return lax.ppermute(x, 'row', [(n, (n + by) % 8) for n in range(8)])  10 us
    pallas_call x4, Pallas kernels, blocks(): pl.pallas_call(functools.partial(next_kernel, shifts), out_shape=(block,)...  4.23 us
    all_to_all x1, starting transfers between devices, on_device(): lax.all_to_all(returned.reshape(peers, 1, ROWS_BACK * LANES), 'obs', 0, 0...  4.04 us
    pallas_call x1, Pallas kernels, on_device(): pl.pallas_call(owner_kernel, out_shape=jax.ShapeDtypeStruct((peers * ROWS...  2.28 us
    pallas_call x1, Pallas kernels, on_device(): pl.pallas_call(pack_kernel, out_shape=jax.ShapeDtypeStruct((peers * ROWS_...  1.84 us
  transfers between devices with their start and end apart: 8, of which 4 were waited for; matrix products, arithmetic and copies ran while one was open for 0% of the time, Pallas kernels for 4%

profile of v4, /device:TPU:32, one launch (start us, length us, event | category | flops | bytes accessed | tf_op | source)
XLA Modules:
  0.0 63.2 jit_solution(9248822475245262068)
XLA Ops:
  0.6 1.8 %pack.1 = f32[256,128]{1,0:T(8,128)S(1)} custom-call(f32[18,1024]{1,0:T(8,128)} %refs_0_.1, f32[6,1024]{1,0:T(8,128)} %refs_1_.1, f32[2,1024]{1,0:T(2,128)} %refs_2_.1, s32[1,1024]{1,0:T(1,128)} %bitcast.10, s32[1,1024]{1,0:T(1,128)} %bitcast.12), custom_call_target="tpu_custom_call" | custom-call | tf_op jit(solution)/shard_map/pack/pallas_call | solution.py:344
  2.5 0.0 copy-start.1
  2.5 15.0 %all_to_all.10 = f32[32,8,128]{2,1,0:T(8,128)S(1)} all-to-all(f32[32,8,128]{2,1,0:T(8,128)S(1)} %bitcast.8), channel_id=1, replica_groups=mesh['obs'=32,'row'=8] {'obs'}, dimensions={0} | all-to-all | bytes 262144 | tf_op jit(solution)/shard_map/all_to_all | solution.py:360
  17.4 0.0 copy-done.1
  17.4 2.3 %owner.1 = f32[1056,128]{1,0:T(8,128)} custom-call(f32[256,128]{1,0:T(8,128)S(1)} %bitcast.9, s32[7,1024]{1,0:T(8,128)S(1)} %copy-done.1), custom_call_target="tpu_custom_call" | custom-call | tf_op jit(solution)/shard_map/owner/pallas_call | solution.py:361
  19.7 0.0 copy-start
  19.7 0.0 copy-start.2
  19.7 0.0 copy-start.3
  19.7 0.0 copy-start.4
  19.7 0.0 copy-start.5
  19.8 4.0 %all-to-all-start.1 = ((f32[32,1,4224]{2,1,0:T(1,128)}), f32[32,1,4224]{2,1,0:T(1,128)S(1)}, u32[]{:S(2)}, u32[]{:S(2)}) async-start(f32[32,1,4224]{2,1,0:T(1,128)} %bitcast.4), calls=%async_computation.1 | async-start | bytes 1081344 | tf_op jit(solution)/shard_map/all_to_all | solution.py:374
  23.8 0.0 copy-done
  23.8 0.0 copy-done.2
  23.8 0.0 copy-done.3
  23.8 0.0 copy-done.4
  23.8 0.0 copy-done.5
  23.9 0.0 copy-start.6
  23.9 0.5 own.1
  24.3 10.7 %all-to-all-done.1 = f32[32,1,4224]{2,1,0:T(1,128)S(1)} async-done(((f32[32,1,4224]{2,1,0:T(1,128)}), f32[32,1,4224]{2,1,0:T(1,128)S(1)}, u32[]{:S(2)}, u32[]{:S(2)}) %all-to-all-start.1) | async-done | bytes 540704 | tf_op jit(solution)/shard_map/all_to_all | solution.py:374
  35.0 0.0 copy-done.6
  35.0 1.7 %camera_0.1 = (f32[176,128]{1,0:T(8,128)S(1)}, bf16[144,2048]{1,0:T(8,128)(2,1)S(1)}, bf16[144,2048]{1,0:T(8,128)(2,1)S(1)}) custom-call(f32[1056,128]{1,0:T(8,128)S(1)} %bitcast.7, f32[32,1024]{1,0:T(8,128)S(1)} %get-tuple-element.17.own, f32[48,1024]{1,0:T(8,128)S(1)} %get-tuple-element.18.split, s32[7,1024]{1,0:T(8,128)S(1)} %copy-done.6), custom_call_target="tpu_custom_call" | custom-call | flops 4000000000 | bytes 4000000 | tf_op jit(solution)/shard_map/camera_0/pallas_call | solution.py:389
  36.7 1.2 %shard_map.97 = (f32[176,128]{1,0:T(8,128)S(1)}, f32[176,128]{1,0:T(8,128)S(1)}) custom-call(f32[32,1024]{1,0:T(8,128)S(1)} %get-tuple-element.17.own, f32[48,1024]{1,0:T(8,128)S(1)} %get-tuple-element.18.split, bf16[144,2048]{1,0:T(8,128)(2,1)S(1)} %get-tuple-element.19.right_hi, bf16[144,2048]{1,0:T(8,128)(2,1)S(1)} %get-tuple-element.20.right_lo), custom_call_target="tpu_custom_call" | custom-call | flops 4000000000 | bytes 4000000 | tf_op jit(solution)/shard_map/pallas_call | solution.py:399
  37.9 1.2 %shard_map.96 = (f32[176,128]{1,0:T(8,128)S(1)}, f32[176,128]{1,0:T(8,128)S(1)}) custom-call(f32[32,1024]{1,0:T(8,128)S(1)} %get-tuple-element.17.own, f32[48,1024]{1,0:T(8,128)S(1)} %get-tuple-element.18.split, bf16[144,2048]{1,0:T(8,128)(2,1)S(1)} %get-tuple-element.19.right_hi, bf16[144,2048]{1,0:T(8,128)(2,1)S(1)} %get-tuple-element.20.right_lo), custom_call_target="tpu_custom_call" | custom-call | flops 4000000000 | bytes 4000000 | tf_op jit(solution)/shard_map/pallas_call | solution.py:399
  39.1 0.2 collective-permute-start.5
  39.3 1.9 %collective-permute-start.2 = (f32[176,128]{1,0:T(8,128)S(1)}, f32[176,128]{1,0:T(8,128)S(1)}, u32[]{:S(2)}, u32[]{:S(2)}) collective-permute-start(f32[176,128]{1,0:T(8,128)S(1)} %get-tuple-element.24), channel_id=1, source_target_pairs={{0,1},{1,2},{2,3},{3,4},{4,5},{5,6},{6,7},{7,0},{8,9},{9,10},{10,1... | collective-permute-start | bytes 270344 | tf_op jit(solution)/shard_map/ppermute | solution.py:408
  41.2 4.5 %collective-permute-start.3 = (f32[176,128]{1,0:T(8,128)S(1)}, f32[176,128]{1,0:T(8,128)S(1)}, u32[]{:S(2)}, u32[]{:S(2)}) collective-permute-start(f32[176,128]{1,0:T(8,128)S(1)} %get-tuple-element.25), channel_id=1, source_target_pairs={{0,2},{1,3},{2,4},{3,5},{4,6},{5,7},{6,0},{7,1},{8,10},{9,11},{10,... | collective-permute-start | bytes 270344 | tf_op jit(solution)/shard_map/ppermute | solution.py:408
  45.7 1.2 %shard_map.95 = (f32[176,128]{1,0:T(8,128)S(1)}, f32[176,128]{1,0:T(8,128)S(1)}) custom-call(f32[32,1024]{1,0:T(8,128)S(1)} %get-tuple-element.17.own, f32[48,1024]{1,0:T(8,128)S(1)} %get-tuple-element.18.split, bf16[144,2048]{1,0:T(8,128)(2,1)S(1)} %get-tuple-element.19.right_hi, bf16[144,2048]{1,0:T(8,128)(2,1)S(1)} %get-tuple-element.20.right_lo), custom_call_target="tpu_custom_call" | custom-call | flops 4000000000 | bytes 4000000 | tf_op jit(solution)/shard_map/pallas_call | solution.py:399
  46.8 2.0 %collective-permute-start = (f32[176,128]{1,0:T(8,128)S(1)}, f32[176,128]{1,0:T(8,128)S(1)}, u32[]{:S(2)}, u32[]{:S(2)}) collective-permute-start(f32[176,128]{1,0:T(8,128)S(1)} %get-tuple-element.21), channel_id=1, source_target_pairs={{0,1},{1,2},{2,3},{3,4},{4,5},{5,6},{6,7},{7,0},{8,9},{9,10},{10,1... | collective-permute-start | bytes 270344 | tf_op jit(solution)/shard_map/ppermute | solution.py:408
  48.8 0.1 collective-permute-start.1
  48.9 0.0 collective-permute-done.5
  49.0 2.2 %collective-permute-start.6 = (f32[176,128]{1,0:T(8,128)S(1)}, f32[176,128]{1,0:T(8,128)S(1)}, u32[]{:S(2)}, u32[]{:S(2)}) collective-permute-start(f32[176,128]{1,0:T(8,128)S(1)} %add.11), channel_id=1, source_target_pairs={{0,6},{1,7},{2,0},{3,1},{4,2},{5,3},{6,4},{7,5},{8,14},{9,15},{10,... | collective-permute-start | bytes 270344 | tf_op jit(solution)/shard_map/ppermute | solution.py:408
  51.2 0.0 collective-permute-done.2
  51.2 3.9 %collective-permute-done.3 = f32[176,128]{1,0:T(8,128)S(1)} collective-permute-done((f32[176,128]{1,0:T(8,128)S(1)}, f32[176,128]{1,0:T(8,128)S(1)}, u32[]{:S(2)}, u32[]{:S(2)}) %collective-permute-start.3) | collective-permute-done | bytes 90144 | tf_op jit(solution)/shard_map/ppermute | solution.py:408
  55.1 0.1 collective-permute-start.4
  55.2 0.7 %shard_map.94.own = f32[176,128]{1,0:T(8,128)S(1)} custom-call(f32[32,1024]{1,0:T(8,128)S(1)} %get-tuple-element.17.own, f32[48,1024]{1,0:T(8,128)S(1)} %get-tuple-element.18.split, bf16[144,2048]{1,0:T(8,128)(2,1)S(1)} %get-tuple-element.19.right_hi, bf16[144,2048]{1,0:T(8,128)(2,1)S(1)} %get-tuple-element.20.right_lo), custom_call_target="tpu_custom_call" | custom-call | flops 4000000000 | bytes 4000000 | tf_op jit(solution)/shard_map/pallas_call | solution.py:399
  55.9 0.0 collective-permute-done.plus1
  56.0 0.0 collective-permute-done.1.minus1
  56.0 0.1 collective-permute-done.6.minus2
  56.1 6.0 %collective-permute-done.4.plus2 = f32[176,128]{1,0:T(8,128)S(1)} collective-permute-done((f32[176,128]{1,0:T(8,128)S(1)}, f32[176,128]{1,0:T(8,128)S(1)}, u32[]{:S(2)}, u32[]{:S(2)}) %collective-permute-start.4) | collective-permute-done | bytes 90144 | tf_op jit(solution)/shard_map/ppermute | solution.py:408
  62.1 1.1 %final.1 = (f32[16,81]{1,0:T(8,128)}, f32[9,16]{1,0:T(8,128)}, f32[81,224]{1,0:T(8,128)}) custom-call(f32[176,128]{1,0:T(8,128)S(1)} %shard_map.94.own, f32[176,128]{1,0:T(8,128)S(1)} %collective-permute-done.plus1, f32[176,128]{1,0:T(8,128)S(1)} %collective-permute-done.1.minus1, f32[176,128]{1,0:T(8,128)S(1)} %collective-permute-done.4.plus2, ...), custom_call_target="tpu_custom_call" | custom-call | tf_op jit(solution)/shard_map/final/pallas_call | solution.py:419
  (2 shorter events, 0.0 us)
Async XLA Ops:
  2.5 15.0 %copy-start.1 = (s32[7,1024]{1,0:T(8,128)S(1)}, s32[7,1024]{1,0:T(8,128)}, u32[]{:S(2)}) copy-start(s32[7,1024]{1,0:T(8,128)} %partner.1) | copy-start | bytes 86020
  19.7 4.1 %copy-start = (f32[18,1024]{1,0:T(8,128)S(1)}, f32[18,1024]{1,0:T(8,128)}, u32[]{:S(2)}) copy-start(f32[18,1024]{1,0:T(8,128)} %refs_0_.1) | copy-start | bytes 221188
  19.7 4.1 %copy-start.2 = (f32[6,1024]{1,0:T(8,128)S(1)}, f32[6,1024]{1,0:T(8,128)}, u32[]{:S(2)}) copy-start(f32[6,1024]{1,0:T(8,128)} %refs_1_.1) | copy-start | bytes 73732
  19.7 4.1 %copy-start.3 = (f32[2,1024]{1,0:T(2,128)S(1)}, f32[2,1024]{1,0:T(2,128)}, u32[]{:S(2)}) copy-start(f32[2,1024]{1,0:T(2,128)} %refs_2_.1) | copy-start | bytes 24580
  19.7 4.1 %copy-start.4 = (s32[1024]{0:T(1024)S(1)}, s32[1024]{0:T(1024)}, u32[]{:S(2)}) copy-start(s32[1024]{0:T(1024)} %param.12) | copy-start | bytes 12292
  19.7 4.1 %copy-start.5 = (s32[1024]{0:T(1024)S(1)}, s32[1024]{0:T(1024)}, u32[]{:S(2)}) copy-start(s32[1024]{0:T(1024)} %param.11) | copy-start | bytes 12292
  19.8 15.3 %all-to-all-start.1 = ((f32[32,1,4224]{2,1,0:T(1,128)}), f32[32,1,4224]{2,1,0:T(1,128)S(1)}, u32[]{:S(2)}, u32[]{:S(2)}) async-start(f32[32,1,4224]{2,1,0:T(1,128)} %bitcast.4), calls=%async_computation.1 | async-start | bytes 1081344 | tf_op jit(solution)/shard_map/all_to_all | solution.py:374
  23.9 11.2 %copy-start.6 = (s32[7,1024]{1,0:T(8,128)S(1)}, s32[7,1024]{1,0:T(8,128)}, u32[]{:S(2)}) copy-start(s32[7,1024]{1,0:T(8,128)} %pair_slot.1) | copy-start | bytes 86020
  39.1 9.8 %collective-permute-start.5 = (f32[176,128]{1,0:T(8,128)S(1)}, f32[176,128]{1,0:T(8,128)S(1)}, u32[]{:S(2)}, u32[]{:S(2)}) collective-permute-start(f32[176,128]{1,0:T(8,128)S(1)} %get-tuple-element.27), channel_id=1, source_target_pairs={{0,7},{1,0},{2,1},{3,2},{4,3},{5,4},{6,5},{7,6},{8,15},{9,8},{10,9... | collective-permute-start | bytes 270344 | tf_op jit(solution)/shard_map/ppermute | solution.py:408
  39.3 11.9 %collective-permute-start.2 = (f32[176,128]{1,0:T(8,128)S(1)}, f32[176,128]{1,0:T(8,128)S(1)}, u32[]{:S(2)}, u32[]{:S(2)}) collective-permute-start(f32[176,128]{1,0:T(8,128)S(1)} %get-tuple-element.24), channel_id=1, source_target_pairs={{0,1},{1,2},{2,3},{3,4},{4,5},{5,6},{6,7},{7,0},{8,9},{9,10},{10,1... | collective-permute-start | bytes 270344 | tf_op jit(solution)/shard_map/ppermute | solution.py:408
  41.2 13.9 %collective-permute-start.3 = (f32[176,128]{1,0:T(8,128)S(1)}, f32[176,128]{1,0:T(8,128)S(1)}, u32[]{:S(2)}, u32[]{:S(2)}) collective-permute-start(f32[176,128]{1,0:T(8,128)S(1)} %get-tuple-element.25), channel_id=1, source_target_pairs={{0,2},{1,3},{2,4},{3,5},{4,6},{5,7},{6,0},{7,1},{8,10},{9,11},{10,... | collective-permute-start | bytes 270344 | tf_op jit(solution)/shard_map/ppermute | solution.py:408
  46.8 9.1 %collective-permute-start = (f32[176,128]{1,0:T(8,128)S(1)}, f32[176,128]{1,0:T(8,128)S(1)}, u32[]{:S(2)}, u32[]{:S(2)}) collective-permute-start(f32[176,128]{1,0:T(8,128)S(1)} %get-tuple-element.21), channel_id=1, source_target_pairs={{0,1},{1,2},{2,3},{3,4},{4,5},{5,6},{6,7},{7,0},{8,9},{9,10},{10,1... | collective-permute-start | bytes 270344 | tf_op jit(solution)/shard_map/ppermute | solution.py:408
  48.8 7.1 %collective-permute-start.1 = (f32[176,128]{1,0:T(8,128)S(1)}, f32[176,128]{1,0:T(8,128)S(1)}, u32[]{:S(2)}, u32[]{:S(2)}) collective-permute-start(f32[176,128]{1,0:T(8,128)S(1)} %get-tuple-element.22), channel_id=1, source_target_pairs={{0,7},{1,0},{2,1},{3,2},{4,3},{5,4},{6,5},{7,6},{8,15},{9,8},{10,9... | collective-permute-start | bytes 270344 | tf_op jit(solution)/shard_map/ppermute | solution.py:408
  49.0 7.1 %collective-permute-start.6 = (f32[176,128]{1,0:T(8,128)S(1)}, f32[176,128]{1,0:T(8,128)S(1)}, u32[]{:S(2)}, u32[]{:S(2)}) collective-permute-start(f32[176,128]{1,0:T(8,128)S(1)} %add.11), channel_id=1, source_target_pairs={{0,6},{1,7},{2,0},{3,1},{4,2},{5,3},{6,4},{7,5},{8,14},{9,15},{10,... | collective-permute-start | bytes 270344 | tf_op jit(solution)/shard_map/ppermute | solution.py:408
  55.1 6.9 %collective-permute-start.4 = (f32[176,128]{1,0:T(8,128)S(1)}, f32[176,128]{1,0:T(8,128)S(1)}, u32[]{:S(2)}, u32[]{:S(2)}) collective-permute-start(f32[176,128]{1,0:T(8,128)S(1)} %add_add_fusion), channel_id=1, source_target_pairs={{0,2},{1,3},{2,4},{3,5},{4,6},{5,7},{6,0},{7,1},{8,10},{9,11},{10,... | collective-permute-start | bytes 270344 | tf_op jit(solution)/shard_map/ppermute | solution.py:408

commit v5 on v4

--- a/solution.py
+++ b/solution.py
@@ -62,7 +62,7 @@
 
 
 def pack_kernel(*refs):
-    sources, (msg, rows, *targets, sems) = refs[:5], refs[5:]
+    sources, (msg, own, split, rows, *targets, sems) = refs[:5], refs[5:]
     copies = [pltpu.make_async_copy(x, y, sems.at[n]) for n, (x, y) in enumerate(zip(sources, targets))]
     for copy in copies:
         copy.start()
@@ -72,25 +72,19 @@
     fill_rows(jc, jp, err, cam, rows)
     group = lane_groups()
     for d in range(CHUNKS):
+        cols = slice(d * LANES, (d + 1) * LANES)
         tiles = [ordered(rows, order, d, t) for t in range(4)]
-        for m, tile in enumerate(regroup(tiles, group)):
-            msg[(d * 4 + m) * ROWS_IN : (d * 4 + m) * ROWS_IN + 8, :] = tile
-
-
-def own_kernel(jc, jp, err, cam, order, own, split, rows):
-    fill_rows(jc, jp, err, cam, rows)
-    for d in range(CHUNKS):
-        cols = slice(d * LANES, (d + 1) * LANES)
-        for t in range(4):
-            value = ordered(rows, order, d, t)
+        for t, value in enumerate(tiles):
             own[t * 8 : t * 8 + 8, cols] = value
             if t < 3:
                 hi = value.astype(BF16).astype(F32)
                 split[t * 8 : t * 8 + 8, cols] = hi
                 split[24 + t * 8 : 32 + t * 8, cols] = (value - hi).astype(BF16).astype(F32)
-
-
-def owner_kernel(owned, partner, msg, slots, turned, near, mixed, back):
+        for m, tile in enumerate(regroup(tiles, group)):
+            msg[(d * 4 + m) * ROWS_IN : (d * 4 + m) * ROWS_IN + 8, :] = tile
+
+
+def owner_kernel(owned, partner, msg, slots, turned, near, mixed, back, plan):
     group = lane_groups()
     for r in range(8):
         slots[pl.ds(r, RANKS, stride=8), :] = partner[:, r * LANES : (r + 1) * LANES]
@@ -117,11 +111,15 @@
         apart = (idx // GROUP - source) & 31
         ranks.append(apart & 7)
         words.append((idx & 31) + jnp.where(apart < 16, GROUP, 0))
-
-    def picks(j):
+        plan[k] = ranks[k]
+    for j in range(1, 8):
         word = jnp.full(TILE, -1, jnp.int32)
         for k in range(RANKS):
             word = jnp.where(ranks[k] == j, words[k], word)
+        plan[6 + j] = word
+
+    def picks(j):
+        word = plan[6 + j]
         return word >= 0, group * GROUP + (word & 31), word >= GROUP
 
     def pick(u, j, lane, ahead):
@@ -165,12 +163,12 @@
 
     h = forward(b0, b1, b2)
     g = [forward(*mine[0:3]), forward(*mine[3:6])]
-    back[126] = inner(g[0], g[0])
-    back[127] = inner(g[0], g[1])
-    back[128] = inner(g[1], g[1])
-    back[129] = inner(g[0], h)
-    back[130] = inner(g[1], h)
-    back[131] = jnp.zeros(TILE, F32)
+    back[0] = inner(g[0], g[0])
+    back[1] = inner(g[0], g[1])
+    back[2] = inner(g[1], g[1])
+    back[3] = inner(g[0], h)
+    back[4] = inner(g[1], h)
+    back[5] = jnp.zeros(TILE, F32)
 
     for j in range(1, 8):
         _, lane, ahead = picks(j)
@@ -182,15 +180,19 @@
             c1 = pick(9 + q, j, lane, ahead)
             for a in range(2):
                 mixed[(j - 1) * 18 + a * 9 + q] = mix[a][0] * c0 + mix[a][1] * c1
-    for k in range(RANKS):
-        hits = [ranks[k] == j for j in range(1, 8)]
-        for n in range(18):
-            out = jnp.zeros(TILE, F32)
-            for j in range(7):
-                out = jnp.where(hits[j], mixed[j * 18 + n], out)
-            back[k * 18 + n] = out
+
+    def ranked(u):
+        k, n = divmod(u, 18)
+        if k >= RANKS:
+            return back[n]
+        rank = plan[k]
+        out = jnp.zeros(TILE, F32)
+        for j in range(7):
+            out = jnp.where(rank == j + 1, mixed[j * 18 + n], out)
+        return out
+
     for row in range(ROWS_BACK):
-        tiles = [back[row * 4 + t] for t in range(4)]
+        tiles = [ranked(row * 4 + t) for t in range(4)]
         tiles = [pltpu.roll(tile, t * GROUP, 1) if t else tile for t, tile in enumerate(tiles)]
         for m in range(4):
             out = tiles[0]
@@ -341,9 +343,13 @@
     peers = lax.axis_size("obs")
     order = send_order.reshape(1, SLOTS)
     raw = (camera_jacobian, point_jacobian, residual, camera_of.reshape(1, SLOTS), order)
-    msg = pl.pallas_call(
+    msg, own, split = pl.pallas_call(
         pack_kernel,
-        out_shape=jax.ShapeDtypeStruct((peers * ROWS_IN, LANES), F32),
+        out_shape=(
+            jax.ShapeDtypeStruct((peers * ROWS_IN, LANES), F32),
+            jax.ShapeDtypeStruct((32, SLOTS), F32),
+            jax.ShapeDtypeStruct((48, SLOTS), F32),
+        ),
         in_specs=[pl.BlockSpec(memory_space=pltpu.HBM)] * 5,
         scratch_shapes=[
             pltpu.VMEM((32, SLOTS), F32),
@@ -366,7 +372,8 @@
             pltpu.VMEM((8 * 52, 8, LANES), F32),
             pltpu.VMEM((RANKS * 6, 8, LANES), F32),
             pltpu.VMEM((RANKS * 18, 8, LANES), F32),
-            pltpu.VMEM((132, 8, LANES), F32),
+            pltpu.VMEM((6, 8, LANES), F32),
+            pltpu.VMEM((14, 8, LANES), jnp.int32),
         ],
         compiler_params=PARAMS,
         name="owner",
@@ -374,14 +381,6 @@
     back = lax.all_to_all(returned.reshape(peers, 1, ROWS_BACK * LANES), "obs", 0, 0, tiled=True)
     block = jax.ShapeDtypeStruct((BLOCK, LANES), F32)
     side = jax.ShapeDtypeStruct((SIDE, 2 * SLOTS), BF16)
-    own, split = pl.pallas_call(
-        own_kernel,
-        out_shape=(jax.ShapeDtypeStruct((32, SLOTS), F32), jax.ShapeDtypeStruct((48, SLOTS), F32)),
-        scratch_shapes=[pltpu.VMEM((32, SLOTS), F32)],
-        compiler_params=PARAMS,
-        cost_estimate=COST,
-        name="own",
-    )(*raw)
 
     def scratch(count):
         return [pltpu.VMEM((2 * count * SIDE, 2 * SLOTS), BF16), pltpu.VMEM((SIDE, LANES), F32)]

time: 63.5 us -> 62 us (0.976)
  blocking collectives: 15 us -> 29.6 us
  waiting for transfers between devices: 20.7 us -> 10 us
  starting transfers between devices: 15 us -> 11 us
  Pallas kernels: 11.6 us -> 10.3 us
    all_to_all x0 -> x1, blocking collectives: none -> 14.6 us  [on_device(): lax.all_to_all(returned.reshape(peers, 1, ROWS_BACK * LANES), 'obs', 0, 0...]
    all_to_all x1 -> x0, waiting for transfers between devices: 10.7 us -> none  [on_device(): lax.all_to_all(returned.reshape(peers, 1, ROWS_BACK * LANES), 'obs', 0, 0...]
    all_to_all x1 -> x0, starting transfers between devices: 4.04 us -> none  [on_device(): lax.all_to_all(returned.reshape(peers, 1, ROWS_BACK * LANES), 'obs', 0, 0...]
    pallas_call x1, Pallas kernels: 2.28 us -> 1.47 us  [on_device(): pl.pallas_call(owner_kernel, out_shape=jax.ShapeDtypeStruct((peers * ROWS...]
    pallas_call x2 -> x1, Pallas kernels: 2.3 us -> 1.84 us  [on_device(): pl.pallas_call(pack_kernel, out_shape=(jax.ShapeDtypeStruct((peers * ROWS...]
  transfers between devices with their start and end apart: 8 -> 7, of which waited for: 4 -> 3; matrix products, arithmetic and copies ran while one was open for 0% -> 0% of each run, Pallas kernels for 4% -> 3%
where the time goes in v5:
time: 62 us; the launch traced here: 61.7 us
  blocking collectives  29.6 us (48%)
  starting transfers between devices  11 us (18%)
  Pallas kernels  10.3 us (17%)
  waiting for transfers between devices  10 us (16%)
  between operations  0.7 us (1%)
    all_to_all x1, blocking collectives, on_device(): lax.all_to_all(msg.reshape(peers, ROWS_IN, LANES), 'obs', 0, 0, tiled=True)  15 us
    all_to_all x1, blocking collectives, on_device(): lax.all_to_all(returned.reshape(peers, 1, ROWS_BACK * LANES), 'obs', 0, 0...  14.6 us
    ppermute x7, starting transfers between devices, shift(): return lax.ppermute(x, 'row', [(n, (n + by) % 8) for n in range(8)])  11 us
    ppermute x7, waiting for transfers between devices, shift(): return lax.ppermute(x, 'row', [(n, (n + by) % 8) for n in range(8)])  10 us
    pallas_call x4, Pallas kernels, blocks(): pl.pallas_call(functools.partial(next_kernel, shifts), out_shape=(block,)...  4.2 us
    pallas_call x1, Pallas kernels, on_device(): pl.pallas_call(pack_kernel, out_shape=(jax.ShapeDtypeStruct((peers * ROWS...  1.84 us
    pallas_call x1, Pallas kernels, on_device(): pl.pallas_call(first_kernel, out_shape=(block, side, side), scratch_shape...  1.73 us
    pallas_call x1, Pallas kernels, on_device(): pl.pallas_call(owner_kernel, out_shape=jax.ShapeDtypeStruct((peers * ROWS...  1.47 us
  transfers between devices with their start and end apart: 7, of which 3 were waited for; matrix products, arithmetic and copies ran while one was open for 0% of the time, Pallas kernels for 3%

profile of v5, /device:TPU:32, one launch (start us, length us, event | category | flops | bytes accessed | tf_op | source)
XLA Modules:
  0.0 61.7 jit_solution(17695633811636003690)
XLA Ops:
  0.6 1.8 %pack.1 = (f32[256,128]{1,0:T(8,128)S(1)}, f32[32,1024]{1,0:T(8,128)S(1)}, f32[48,1024]{1,0:T(8,128)S(1)}) custom-call(f32[18,1024]{1,0:T(8,128)} %refs_0_.1, f32[6,1024]{1,0:T(8,128)} %refs_1_.1, f32[2,1024]{1,0:T(2,128)} %refs_2_.1, s32[1,1024]{1,0:T(1,128)} %bitcast.11, s32[1,1024]{1,0:T(1,128)} %bitcast.12), custom_call_target="tpu_custom_call" | custom-call | tf_op jit(solution)/shard_map/pack/pallas_call | solution.py:346
  2.5 0.0 copy-start
  2.5 15.0 %all_to_all.10 = f32[32,8,128]{2,1,0:T(8,128)S(1)} all-to-all(f32[32,8,128]{2,1,0:T(8,128)S(1)} %bitcast.10), channel_id=1, replica_groups=mesh['obs'=32,'row'=8] {'obs'}, dimensions={0} | all-to-all | bytes 262144 | tf_op jit(solution)/shard_map/all_to_all | solution.py:366
  17.4 0.0 copy-done
  17.4 1.5 %owner.1 = f32[1056,128]{1,0:T(8,128)S(1)} custom-call(f32[256,128]{1,0:T(8,128)S(1)} %bitcast.9, s32[7,1024]{1,0:T(8,128)S(1)} %copy-done), custom_call_target="tpu_custom_call" | custom-call | tf_op jit(solution)/shard_map/owner/pallas_call | solution.py:367
  18.9 0.0 copy-start.1
  18.9 14.6 %all_to_all.11 = f32[32,1,4224]{2,1,0:T(1,128)S(1)} all-to-all(f32[32,1,4224]{2,1,0:T(1,128)S(1)} %bitcast.7), channel_id=1, replica_groups=mesh['obs'=32,'row'=8] {'obs'}, dimensions={0} | all-to-all | bytes 1081344 | tf_op jit(solution)/shard_map/all_to_all | solution.py:381
  33.6 0.0 copy-done.1
  33.6 1.7 %camera_0.1 = (f32[176,128]{1,0:T(8,128)S(1)}, bf16[144,2048]{1,0:T(8,128)(2,1)S(1)}, bf16[144,2048]{1,0:T(8,128)(2,1)S(1)}) custom-call(f32[1056,128]{1,0:T(8,128)S(1)} %bitcast.8, f32[32,1024]{1,0:T(8,128)S(1)} %get-tuple-element.18.own, f32[48,1024]{1,0:T(8,128)S(1)} %get-tuple-element.19.split, s32[7,1024]{1,0:T(8,128)S(1)} %copy-done.1), custom_call_target="tpu_custom_call" | custom-call | flops 4000000000 | bytes 4000000 | tf_op jit(solution)/shard_map/camera_0/pallas_call | solution.py:388
  35.3 1.2 %shard_map.97 = (f32[176,128]{1,0:T(8,128)S(1)}, f32[176,128]{1,0:T(8,128)S(1)}) custom-call(f32[32,1024]{1,0:T(8,128)S(1)} %get-tuple-element.18.own, f32[48,1024]{1,0:T(8,128)S(1)} %get-tuple-element.19.split, bf16[144,2048]{1,0:T(8,128)(2,1)S(1)} %get-tuple-element.21.right_hi, bf16[144,2048]{1,0:T(8,128)(2,1)S(1)} %get-tuple-element.22.right_lo), custom_call_target="tpu_custom_call" | custom-call | flops 4000000000 | bytes 4000000 | tf_op jit(solution)/shard_map/pallas_call | solution.py:398
  36.5 1.2 %shard_map.96 = (f32[176,128]{1,0:T(8,128)S(1)}, f32[176,128]{1,0:T(8,128)S(1)}) custom-call(f32[32,1024]{1,0:T(8,128)S(1)} %get-tuple-element.18.own, f32[48,1024]{1,0:T(8,128)S(1)} %get-tuple-element.19.split, bf16[144,2048]{1,0:T(8,128)(2,1)S(1)} %get-tuple-element.21.right_hi, bf16[144,2048]{1,0:T(8,128)(2,1)S(1)} %get-tuple-element.22.right_lo), custom_call_target="tpu_custom_call" | custom-call | flops 4000000000 | bytes 4000000 | tf_op jit(solution)/shard_map/pallas_call | solution.py:398
  37.6 0.2 collective-permute-start.5
  37.8 1.9 %collective-permute-start.2 = (f32[176,128]{1,0:T(8,128)S(1)}, f32[176,128]{1,0:T(8,128)S(1)}, u32[]{:S(2)}, u32[]{:S(2)}) collective-permute-start(f32[176,128]{1,0:T(8,128)S(1)} %get-tuple-element.26), channel_id=1, source_target_pairs={{0,1},{1,2},{2,3},{3,4},{4,5},{5,6},{6,7},{7,0},{8,9},{9,10},{10,1... | collective-permute-start | bytes 270344 | tf_op jit(solution)/shard_map/ppermute | solution.py:407
  39.7 4.5 %collective-permute-start.3 = (f32[176,128]{1,0:T(8,128)S(1)}, f32[176,128]{1,0:T(8,128)S(1)}, u32[]{:S(2)}, u32[]{:S(2)}) collective-permute-start(f32[176,128]{1,0:T(8,128)S(1)} %get-tuple-element.27), channel_id=1, source_target_pairs={{0,2},{1,3},{2,4},{3,5},{4,6},{5,7},{6,0},{7,1},{8,10},{9,11},{10,... | collective-permute-start | bytes 270344 | tf_op jit(solution)/shard_map/ppermute | solution.py:407
  44.2 1.2 %shard_map.95 = (f32[176,128]{1,0:T(8,128)S(1)}, f32[176,128]{1,0:T(8,128)S(1)}) custom-call(f32[32,1024]{1,0:T(8,128)S(1)} %get-tuple-element.18.own, f32[48,1024]{1,0:T(8,128)S(1)} %get-tuple-element.19.split, bf16[144,2048]{1,0:T(8,128)(2,1)S(1)} %get-tuple-element.21.right_hi, bf16[144,2048]{1,0:T(8,128)(2,1)S(1)} %get-tuple-element.22.right_lo), custom_call_target="tpu_custom_call" | custom-call | flops 4000000000 | bytes 4000000 | tf_op jit(solution)/shard_map/pallas_call | solution.py:398
  45.4 2.0 %collective-permute-start = (f32[176,128]{1,0:T(8,128)S(1)}, f32[176,128]{1,0:T(8,128)S(1)}, u32[]{:S(2)}, u32[]{:S(2)}) collective-permute-start(f32[176,128]{1,0:T(8,128)S(1)} %get-tuple-element.23), channel_id=1, source_target_pairs={{0,1},{1,2},{2,3},{3,4},{4,5},{5,6},{6,7},{7,0},{8,9},{9,10},{10,1... | collective-permute-start | bytes 270344 | tf_op jit(solution)/shard_map/ppermute | solution.py:407
  47.4 0.1 collective-permute-start.1
  47.5 0.0 collective-permute-done.5
  47.5 2.2 %collective-permute-start.6 = (f32[176,128]{1,0:T(8,128)S(1)}, f32[176,128]{1,0:T(8,128)S(1)}, u32[]{:S(2)}, u32[]{:S(2)}) collective-permute-start(f32[176,128]{1,0:T(8,128)S(1)} %add.11), channel_id=1, source_target_pairs={{0,6},{1,7},{2,0},{3,1},{4,2},{5,3},{6,4},{7,5},{8,14},{9,15},{10,... | collective-permute-start | bytes 270344 | tf_op jit(solution)/shard_map/ppermute | solution.py:407
  49.8 0.0 collective-permute-done.2
  49.8 3.9 %collective-permute-done.3 = f32[176,128]{1,0:T(8,128)S(1)} collective-permute-done((f32[176,128]{1,0:T(8,128)S(1)}, f32[176,128]{1,0:T(8,128)S(1)}, u32[]{:S(2)}, u32[]{:S(2)}) %collective-permute-start.3) | collective-permute-done | bytes 90144 | tf_op jit(solution)/shard_map/ppermute | solution.py:407
  53.7 0.1 collective-permute-start.4
  53.8 0.7 %shard_map.94.own = f32[176,128]{1,0:T(8,128)S(1)} custom-call(f32[32,1024]{1,0:T(8,128)S(1)} %get-tuple-element.18.own, f32[48,1024]{1,0:T(8,128)S(1)} %get-tuple-element.19.split, bf16[144,2048]{1,0:T(8,128)(2,1)S(1)} %get-tuple-element.21.right_hi, bf16[144,2048]{1,0:T(8,128)(2,1)S(1)} %get-tuple-element.22.right_lo), custom_call_target="tpu_custom_call" | custom-call | flops 4000000000 | bytes 4000000 | tf_op jit(solution)/shard_map/pallas_call | solution.py:398
  54.5 0.0 collective-permute-done.plus1
  54.5 0.0 collective-permute-done.1.minus1
  54.5 0.1 collective-permute-done.6.minus2
  54.6 6.0 %collective-permute-done.4.plus2 = f32[176,128]{1,0:T(8,128)S(1)} collective-permute-done((f32[176,128]{1,0:T(8,128)S(1)}, f32[176,128]{1,0:T(8,128)S(1)}, u32[]{:S(2)}, u32[]{:S(2)}) %collective-permute-start.4) | collective-permute-done | bytes 90144 | tf_op jit(solution)/shard_map/ppermute | solution.py:407
  60.6 1.1 %final.1 = (f32[16,81]{1,0:T(8,128)}, f32[9,16]{1,0:T(8,128)}, f32[81,224]{1,0:T(8,128)}) custom-call(f32[176,128]{1,0:T(8,128)S(1)} %shard_map.94.own, f32[176,128]{1,0:T(8,128)S(1)} %collective-permute-done.plus1, f32[176,128]{1,0:T(8,128)S(1)} %collective-permute-done.1.minus1, f32[176,128]{1,0:T(8,128)S(1)} %collective-permute-done.4.plus2, ...), custom_call_target="tpu_custom_call" | custom-call | tf_op jit(solution)/shard_map/final/pallas_call | solution.py:418
  (2 shorter events, 0.0 us)
Async XLA Ops:
  2.5 15.0 %copy-start = (s32[7,1024]{1,0:T(8,128)S(1)}, s32[7,1024]{1,0:T(8,128)}, u32[]{:S(2)}) copy-start(s32[7,1024]{1,0:T(8,128)} %partner.1) | copy-start | bytes 86020
  18.9 14.7 %copy-start.1 = (s32[7,1024]{1,0:T(8,128)S(1)}, s32[7,1024]{1,0:T(8,128)}, u32[]{:S(2)}) copy-start(s32[7,1024]{1,0:T(8,128)} %pair_slot.1) | copy-start | bytes 86020
  37.6 9.8 %collective-permute-start.5 = (f32[176,128]{1,0:T(8,128)S(1)}, f32[176,128]{1,0:T(8,128)S(1)}, u32[]{:S(2)}, u32[]{:S(2)}) collective-permute-start(f32[176,128]{1,0:T(8,128)S(1)} %get-tuple-element.29), channel_id=1, source_target_pairs={{0,7},{1,0},{2,1},{3,2},{4,3},{5,4},{6,5},{7,6},{8,15},{9,8},{10,9... | collective-permute-start | bytes 270344 | tf_op jit(solution)/shard_map/ppermute | solution.py:407
  37.8 11.9 %collective-permute-start.2 = (f32[176,128]{1,0:T(8,128)S(1)}, f32[176,128]{1,0:T(8,128)S(1)}, u32[]{:S(2)}, u32[]{:S(2)}) collective-permute-start(f32[176,128]{1,0:T(8,128)S(1)} %get-tuple-element.26), channel_id=1, source_target_pairs={{0,1},{1,2},{2,3},{3,4},{4,5},{5,6},{6,7},{7,0},{8,9},{9,10},{10,1... | collective-permute-start | bytes 270344 | tf_op jit(solution)/shard_map/ppermute | solution.py:407
  39.7 13.9 %collective-permute-start.3 = (f32[176,128]{1,0:T(8,128)S(1)}, f32[176,128]{1,0:T(8,128)S(1)}, u32[]{:S(2)}, u32[]{:S(2)}) collective-permute-start(f32[176,128]{1,0:T(8,128)S(1)} %get-tuple-element.27), channel_id=1, source_target_pairs={{0,2},{1,3},{2,4},{3,5},{4,6},{5,7},{6,0},{7,1},{8,10},{9,11},{10,... | collective-permute-start | bytes 270344 | tf_op jit(solution)/shard_map/ppermute | solution.py:407
  45.4 9.1 %collective-permute-start = (f32[176,128]{1,0:T(8,128)S(1)}, f32[176,128]{1,0:T(8,128)S(1)}, u32[]{:S(2)}, u32[]{:S(2)}) collective-permute-start(f32[176,128]{1,0:T(8,128)S(1)} %get-tuple-element.23), channel_id=1, source_target_pairs={{0,1},{1,2},{2,3},{3,4},{4,5},{5,6},{6,7},{7,0},{8,9},{9,10},{10,1... | collective-permute-start | bytes 270344 | tf_op jit(solution)/shard_map/ppermute | solution.py:407
  47.4 7.1 %collective-permute-start.1 = (f32[176,128]{1,0:T(8,128)S(1)}, f32[176,128]{1,0:T(8,128)S(1)}, u32[]{:S(2)}, u32[]{:S(2)}) collective-permute-start(f32[176,128]{1,0:T(8,128)S(1)} %get-tuple-element.24), channel_id=1, source_target_pairs={{0,7},{1,0},{2,1},{3,2},{4,3},{5,4},{6,5},{7,6},{8,15},{9,8},{10,9... | collective-permute-start | bytes 270344 | tf_op jit(solution)/shard_map/ppermute | solution.py:407
  47.5 7.1 %collective-permute-start.6 = (f32[176,128]{1,0:T(8,128)S(1)}, f32[176,128]{1,0:T(8,128)S(1)}, u32[]{:S(2)}, u32[]{:S(2)}) collective-permute-start(f32[176,128]{1,0:T(8,128)S(1)} %add.11), channel_id=1, source_target_pairs={{0,6},{1,7},{2,0},{3,1},{4,2},{5,3},{6,4},{7,5},{8,14},{9,15},{10,... | collective-permute-start | bytes 270344 | tf_op jit(solution)/shard_map/ppermute | solution.py:407
  53.7 6.9 %collective-permute-start.4 = (f32[176,128]{1,0:T(8,128)S(1)}, f32[176,128]{1,0:T(8,128)S(1)}, u32[]{:S(2)}, u32[]{:S(2)}) collective-permute-start(f32[176,128]{1,0:T(8,128)S(1)} %add_add_fusion), channel_id=1, source_target_pairs={{0,2},{1,3},{2,4},{3,5},{4,6},{5,7},{6,0},{7,1},{8,10},{9,11},{10,... | collective-permute-start | bytes 270344 | tf_op jit(solution)/shard_map/ppermute | solution.py:407

commit v6 on v5

--- a/solution.py
+++ b/solution.py
@@ -18,7 +18,7 @@
 ROWS_IN = 8
 ROWS_BACK = 33
 SIDE = 144
-BLOCK = 176
+BLOCK = 168
 damping = 1.0
 COST = pl.CostEstimate(flops=4_000_000_000, bytes_accessed=4_000_000, transcendentals=0)
 PARAMS = pltpu.CompilerParams(vmem_limit_bytes=16 << 20)
@@ -284,7 +284,7 @@
         for p in range(1, 8):
             tail = jnp.where(lane // 16 == p, pltpu.roll(wide[p * 16 : p * 16 + 16, :], p * 16, 1), tail)
         out[SIDE : SIDE + 16, :] = tail
-        out[SIDE + 16 : BLOCK, :] = wide[128:144, :]
+        out[SIDE + 16 : BLOCK, :] = jnp.where(lane[:8] // 16 == 1, pltpu.roll(wide[136:144, :], 16, 1), wide[128:136, :])
 
 
 def first_kernel(back, own, split, pair_slot, block, right_hi, right_lo, left, wide, flat):
@@ -304,7 +304,8 @@
     for p in range(8):
         piece = body[SIDE : SIDE + 16, :]
         last[p * 16 : p * 16 + 16, :] = piece if p == 0 else pltpu.roll(piece, (LANES - p * 16) % LANES, 1)
-    last[128:144, :] = body[SIDE + 16 : BLOCK, :]
+    last[128:136, :] = body[SIDE + 16 : BLOCK, :]
+    last[136:144, :] = pltpu.roll(body[SIDE + 16 : BLOCK, :], LANES - 16, 1)
     lane = lax.broadcasted_iota(jnp.int32, (9, LANES), 1)
     grads = jnp.zeros((9, LANES), F32)
     for q in range(9):

time: 62 us -> 61.6 us (level)
  transfers between devices with their start and end apart: 7 -> 7, of which waited for: 3 -> 2; matrix products, arithmetic and copies ran while one was open for 0% -> 0% of each run, Pallas kernels for 3% -> 3%
where the time goes in v6:
time: 61.6 us; the launch traced here: 61.4 us
  blocking collectives  29.6 us (48%)
  starting transfers between devices  11 us (18%)
  Pallas kernels  10.4 us (17%)
  waiting for transfers between devices  9.68 us (16%)
  between operations  0.69 us (1%)
    all_to_all x1, blocking collectives, on_device(): lax.all_to_all(msg.reshape(peers, ROWS_IN, LANES), 'obs', 0, 0, tiled=True)  15 us
    all_to_all x1, blocking collectives, on_device(): lax.all_to_all(returned.reshape(peers, 1, ROWS_BACK * LANES), 'obs', 0, 0...  14.6 us
    ppermute x7, starting transfers between devices, shift(): return lax.ppermute(x, 'row', [(n, (n + by) % 8) for n in range(8)])  11 us
    ppermute x7, waiting for transfers between devices, shift(): return lax.ppermute(x, 'row', [(n, (n + by) % 8) for n in range(8)])  9.68 us
    pallas_call x4, Pallas kernels, blocks(): pl.pallas_call(functools.partial(next_kernel, shifts), out_shape=(block,)...  4.25 us
    pallas_call x1, Pallas kernels, on_device(): pl.pallas_call(pack_kernel, out_shape=(jax.ShapeDtypeStruct((peers * ROWS...  1.84 us
    pallas_call x1, Pallas kernels, on_device(): pl.pallas_call(first_kernel, out_shape=(block, side, side), scratch_shape...  1.74 us
    pallas_call x1, Pallas kernels, on_device(): pl.pallas_call(owner_kernel, out_shape=jax.ShapeDtypeStruct((peers * ROWS...  1.47 us
  transfers between devices with their start and end apart: 7, of which 2 were waited for; matrix products, arithmetic and copies ran while one was open for 0% of the time, Pallas kernels for 3%

profile of v6, /device:TPU:32, one launch (start us, length us, event | category | flops | bytes accessed | tf_op | source)
XLA Modules:
  0.0 61.4 jit_solution(1741215373924046070)
XLA Ops:
  0.6 1.8 %pack.1 = (f32[256,128]{1,0:T(8,128)S(1)}, f32[32,1024]{1,0:T(8,128)S(1)}, f32[48,1024]{1,0:T(8,128)S(1)}) custom-call(f32[18,1024]{1,0:T(8,128)} %refs_0_.1, f32[6,1024]{1,0:T(8,128)} %refs_1_.1, f32[2,1024]{1,0:T(2,128)} %refs_2_.1, s32[1,1024]{1,0:T(1,128)} %bitcast.11, s32[1,1024]{1,0:T(1,128)} %bitcast.12), custom_call_target="tpu_custom_call" | custom-call | tf_op jit(solution)/shard_map/pack/pallas_call | solution.py:347
  2.5 0.0 copy-start
  2.5 15.0 %all_to_all.10 = f32[32,8,128]{2,1,0:T(8,128)S(1)} all-to-all(f32[32,8,128]{2,1,0:T(8,128)S(1)} %bitcast.10), channel_id=1, replica_groups=mesh['obs'=32,'row'=8] {'obs'}, dimensions={0} | all-to-all | bytes 262144 | tf_op jit(solution)/shard_map/all_to_all | solution.py:367
  17.4 0.0 copy-done
  17.4 1.5 %owner.1 = f32[1056,128]{1,0:T(8,128)S(1)} custom-call(f32[256,128]{1,0:T(8,128)S(1)} %bitcast.9, s32[7,1024]{1,0:T(8,128)S(1)} %copy-done), custom_call_target="tpu_custom_call" | custom-call | tf_op jit(solution)/shard_map/owner/pallas_call | solution.py:368
  18.9 0.0 copy-start.1
  18.9 14.6 %all_to_all.11 = f32[32,1,4224]{2,1,0:T(1,128)S(1)} all-to-all(f32[32,1,4224]{2,1,0:T(1,128)S(1)} %bitcast.7), channel_id=1, replica_groups=mesh['obs'=32,'row'=8] {'obs'}, dimensions={0} | all-to-all | bytes 1081344 | tf_op jit(solution)/shard_map/all_to_all | solution.py:382
  33.6 0.0 copy-done.1
  33.6 1.7 %camera_0.1 = (f32[168,128]{1,0:T(8,128)S(1)}, bf16[144,2048]{1,0:T(8,128)(2,1)S(1)}, bf16[144,2048]{1,0:T(8,128)(2,1)S(1)}) custom-call(f32[1056,128]{1,0:T(8,128)S(1)} %bitcast.8, f32[32,1024]{1,0:T(8,128)S(1)} %get-tuple-element.18.own, f32[48,1024]{1,0:T(8,128)S(1)} %get-tuple-element.19.split, s32[7,1024]{1,0:T(8,128)S(1)} %copy-done.1), custom_call_target="tpu_custom_call" | custom-call | flops 4000000000 | bytes 4000000 | tf_op jit(solution)/shard_map/camera_0/pallas_call | solution.py:389
  35.3 1.2 %shard_map.97 = (f32[168,128]{1,0:T(8,128)S(1)}, f32[168,128]{1,0:T(8,128)S(1)}) custom-call(f32[32,1024]{1,0:T(8,128)S(1)} %get-tuple-element.18.own, f32[48,1024]{1,0:T(8,128)S(1)} %get-tuple-element.19.split, bf16[144,2048]{1,0:T(8,128)(2,1)S(1)} %get-tuple-element.21.right_hi, bf16[144,2048]{1,0:T(8,128)(2,1)S(1)} %get-tuple-element.22.right_lo), custom_call_target="tpu_custom_call" | custom-call | flops 4000000000 | bytes 4000000 | tf_op jit(solution)/shard_map/pallas_call | solution.py:399
  36.5 1.2 %shard_map.96 = (f32[168,128]{1,0:T(8,128)S(1)}, f32[168,128]{1,0:T(8,128)S(1)}) custom-call(f32[32,1024]{1,0:T(8,128)S(1)} %get-tuple-element.18.own, f32[48,1024]{1,0:T(8,128)S(1)} %get-tuple-element.19.split, bf16[144,2048]{1,0:T(8,128)(2,1)S(1)} %get-tuple-element.21.right_hi, bf16[144,2048]{1,0:T(8,128)(2,1)S(1)} %get-tuple-element.22.right_lo), custom_call_target="tpu_custom_call" | custom-call | flops 4000000000 | bytes 4000000 | tf_op jit(solution)/shard_map/pallas_call | solution.py:399
  37.7 0.2 collective-permute-start.5
  37.9 1.9 %collective-permute-start.2 = (f32[168,128]{1,0:T(8,128)S(1)}, f32[168,128]{1,0:T(8,128)S(1)}, u32[]{:S(2)}, u32[]{:S(2)}) collective-permute-start(f32[168,128]{1,0:T(8,128)S(1)} %get-tuple-element.26), channel_id=1, source_target_pairs={{0,1},{1,2},{2,3},{3,4},{4,5},{5,6},{6,7},{7,0},{8,9},{9,10},{10,1... | collective-permute-start | bytes 258056 | tf_op jit(solution)/shard_map/ppermute | solution.py:408
  39.8 4.5 %collective-permute-start.3 = (f32[168,128]{1,0:T(8,128)S(1)}, f32[168,128]{1,0:T(8,128)S(1)}, u32[]{:S(2)}, u32[]{:S(2)}) collective-permute-start(f32[168,128]{1,0:T(8,128)S(1)} %get-tuple-element.27), channel_id=1, source_target_pairs={{0,2},{1,3},{2,4},{3,5},{4,6},{5,7},{6,0},{7,1},{8,10},{9,11},{10,... | collective-permute-start | bytes 258056 | tf_op jit(solution)/shard_map/ppermute | solution.py:408
  44.3 1.2 %shard_map.95 = (f32[168,128]{1,0:T(8,128)S(1)}, f32[168,128]{1,0:T(8,128)S(1)}) custom-call(f32[32,1024]{1,0:T(8,128)S(1)} %get-tuple-element.18.own, f32[48,1024]{1,0:T(8,128)S(1)} %get-tuple-element.19.split, bf16[144,2048]{1,0:T(8,128)(2,1)S(1)} %get-tuple-element.21.right_hi, bf16[144,2048]{1,0:T(8,128)(2,1)S(1)} %get-tuple-element.22.right_lo), custom_call_target="tpu_custom_call" | custom-call | flops 4000000000 | bytes 4000000 | tf_op jit(solution)/shard_map/pallas_call | solution.py:399
  45.4 2.0 %collective-permute-start = (f32[168,128]{1,0:T(8,128)S(1)}, f32[168,128]{1,0:T(8,128)S(1)}, u32[]{:S(2)}, u32[]{:S(2)}) collective-permute-start(f32[168,128]{1,0:T(8,128)S(1)} %get-tuple-element.23), channel_id=1, source_target_pairs={{0,1},{1,2},{2,3},{3,4},{4,5},{5,6},{6,7},{7,0},{8,9},{9,10},{10,1... | collective-permute-start | bytes 258056 | tf_op jit(solution)/shard_map/ppermute | solution.py:408
  47.4 0.1 collective-permute-start.1
  47.5 0.0 collective-permute-done.5
  47.6 2.2 %collective-permute-start.6 = (f32[168,128]{1,0:T(8,128)S(1)}, f32[168,128]{1,0:T(8,128)S(1)}, u32[]{:S(2)}, u32[]{:S(2)}) collective-permute-start(f32[168,128]{1,0:T(8,128)S(1)} %add.11), channel_id=1, source_target_pairs={{0,6},{1,7},{2,0},{3,1},{4,2},{5,3},{6,4},{7,5},{8,14},{9,15},{10,... | collective-permute-start | bytes 258056 | tf_op jit(solution)/shard_map/ppermute | solution.py:408
  49.8 0.0 collective-permute-done.2
  49.8 3.7 %collective-permute-done.3 = f32[168,128]{1,0:T(8,128)S(1)} collective-permute-done((f32[168,128]{1,0:T(8,128)S(1)}, f32[168,128]{1,0:T(8,128)S(1)}, u32[]{:S(2)}, u32[]{:S(2)}) %collective-permute-start.3) | collective-permute-done | bytes 86048 | tf_op jit(solution)/shard_map/ppermute | solution.py:408
  53.5 0.1 collective-permute-start.4
  53.6 0.7 %shard_map.94.own = f32[168,128]{1,0:T(8,128)S(1)} custom-call(f32[32,1024]{1,0:T(8,128)S(1)} %get-tuple-element.18.own, f32[48,1024]{1,0:T(8,128)S(1)} %get-tuple-element.19.split, bf16[144,2048]{1,0:T(8,128)(2,1)S(1)} %get-tuple-element.21.right_hi, bf16[144,2048]{1,0:T(8,128)(2,1)S(1)} %get-tuple-element.22.right_lo), custom_call_target="tpu_custom_call" | custom-call | flops 4000000000 | bytes 4000000 | tf_op jit(solution)/shard_map/pallas_call | solution.py:399
  54.3 0.0 collective-permute-done.plus1
  54.3 0.0 collective-permute-done.1.minus1
  54.3 0.0 collective-permute-done.6.minus2
  54.3 5.9 %collective-permute-done.4.plus2 = f32[168,128]{1,0:T(8,128)S(1)} collective-permute-done((f32[168,128]{1,0:T(8,128)S(1)}, f32[168,128]{1,0:T(8,128)S(1)}, u32[]{:S(2)}, u32[]{:S(2)}) %collective-permute-start.4) | collective-permute-done | bytes 86048 | tf_op jit(solution)/shard_map/ppermute | solution.py:408
  60.3 1.1 %final.1 = (f32[16,81]{1,0:T(8,128)}, f32[9,16]{1,0:T(8,128)}, f32[81,224]{1,0:T(8,128)}) custom-call(f32[168,128]{1,0:T(8,128)S(1)} %shard_map.94.own, f32[168,128]{1,0:T(8,128)S(1)} %collective-permute-done.plus1, f32[168,128]{1,0:T(8,128)S(1)} %collective-permute-done.1.minus1, f32[168,128]{1,0:T(8,128)S(1)} %collective-permute-done.4.plus2, ...), custom_call_target="tpu_custom_call" | custom-call | tf_op jit(solution)/shard_map/final/pallas_call | solution.py:419
  (2 shorter events, 0.0 us)
Async XLA Ops:
  2.5 15.0 %copy-start = (s32[7,1024]{1,0:T(8,128)S(1)}, s32[7,1024]{1,0:T(8,128)}, u32[]{:S(2)}) copy-start(s32[7,1024]{1,0:T(8,128)} %partner.1) | copy-start | bytes 86020
  18.9 14.7 %copy-start.1 = (s32[7,1024]{1,0:T(8,128)S(1)}, s32[7,1024]{1,0:T(8,128)}, u32[]{:S(2)}) copy-start(s32[7,1024]{1,0:T(8,128)} %pair_slot.1) | copy-start | bytes 86020
  37.7 9.9 %collective-permute-start.5 = (f32[168,128]{1,0:T(8,128)S(1)}, f32[168,128]{1,0:T(8,128)S(1)}, u32[]{:S(2)}, u32[]{:S(2)}) collective-permute-start(f32[168,128]{1,0:T(8,128)S(1)} %get-tuple-element.29), channel_id=1, source_target_pairs={{0,7},{1,0},{2,1},{3,2},{4,3},{5,4},{6,5},{7,6},{8,15},{9,8},{10,9... | collective-permute-start | bytes 258056 | tf_op jit(solution)/shard_map/ppermute | solution.py:408
  37.9 11.9 %collective-permute-start.2 = (f32[168,128]{1,0:T(8,128)S(1)}, f32[168,128]{1,0:T(8,128)S(1)}, u32[]{:S(2)}, u32[]{:S(2)}) collective-permute-start(f32[168,128]{1,0:T(8,128)S(1)} %get-tuple-element.26), channel_id=1, source_target_pairs={{0,1},{1,2},{2,3},{3,4},{4,5},{5,6},{6,7},{7,0},{8,9},{9,10},{10,1... | collective-permute-start | bytes 258056 | tf_op jit(solution)/shard_map/ppermute | solution.py:408
  39.8 13.7 %collective-permute-start.3 = (f32[168,128]{1,0:T(8,128)S(1)}, f32[168,128]{1,0:T(8,128)S(1)}, u32[]{:S(2)}, u32[]{:S(2)}) collective-permute-start(f32[168,128]{1,0:T(8,128)S(1)} %get-tuple-element.27), channel_id=1, source_target_pairs={{0,2},{1,3},{2,4},{3,5},{4,6},{5,7},{6,0},{7,1},{8,10},{9,11},{10,... | collective-permute-start | bytes 258056 | tf_op jit(solution)/shard_map/ppermute | solution.py:408
  45.4 8.8 %collective-permute-start = (f32[168,128]{1,0:T(8,128)S(1)}, f32[168,128]{1,0:T(8,128)S(1)}, u32[]{:S(2)}, u32[]{:S(2)}) collective-permute-start(f32[168,128]{1,0:T(8,128)S(1)} %get-tuple-element.23), channel_id=1, source_target_pairs={{0,1},{1,2},{2,3},{3,4},{4,5},{5,6},{6,7},{7,0},{8,9},{9,10},{10,1... | collective-permute-start | bytes 258056 | tf_op jit(solution)/shard_map/ppermute | solution.py:408
  47.4 6.9 %collective-permute-start.1 = (f32[168,128]{1,0:T(8,128)S(1)}, f32[168,128]{1,0:T(8,128)S(1)}, u32[]{:S(2)}, u32[]{:S(2)}) collective-permute-start(f32[168,128]{1,0:T(8,128)S(1)} %get-tuple-element.24), channel_id=1, source_target_pairs={{0,7},{1,0},{2,1},{3,2},{4,3},{5,4},{6,5},{7,6},{8,15},{9,8},{10,9... | collective-permute-start | bytes 258056 | tf_op jit(solution)/shard_map/ppermute | solution.py:408
  47.6 6.8 %collective-permute-start.6 = (f32[168,128]{1,0:T(8,128)S(1)}, f32[168,128]{1,0:T(8,128)S(1)}, u32[]{:S(2)}, u32[]{:S(2)}) collective-permute-start(f32[168,128]{1,0:T(8,128)S(1)} %add.11), channel_id=1, source_target_pairs={{0,6},{1,7},{2,0},{3,1},{4,2},{5,3},{6,4},{7,5},{8,14},{9,15},{10,... | collective-permute-start | bytes 258056 | tf_op jit(solution)/shard_map/ppermute | solution.py:408
  53.5 6.8 %collective-permute-start.4 = (f32[168,128]{1,0:T(8,128)S(1)}, f32[168,128]{1,0:T(8,128)S(1)}, u32[]{:S(2)}, u32[]{:S(2)}) collective-permute-start(f32[168,128]{1,0:T(8,128)S(1)} %add_add_fusion), channel_id=1, source_target_pairs={{0,2},{1,3},{2,4},{3,5},{4,6},{5,7},{6,0},{7,1},{8,10},{9,11},{10,... | collective-permute-start | bytes 258056 | tf_op jit(solution)/shard_map/ppermute | solution.py:408
